TPU v7x, 512 devices: a whole 4x8x8 slice. The times are simulated.
512 devices in a mesh: req: 64 (over x, z, core), pre: 8 (over y).
Axes of the slice: x: 4, y: 8, z: 8, core: 2. Of those that a mesh axis runs over, the one named last changes fastest.
Arguments:
- queries_raw: bfloat16 [16384, 3072], P('req', 'pre'), may hold values from -60 to 60
- keys_raw: bfloat16 [16384, 3072], P('req', 'pre'), may hold values from -60 to 60
- values: bfloat16 [16384, 3072], P('req', 'pre'), may hold values from -6 to 6
- query_gain: float32 [3072], P('pre'), may hold values from 1 to 3
- key_gain: float32 [3072], P('pre'), may hold values from 1 to 3
- prefix_keys: bfloat16 [8192, 3072], P('req', 'pre'), may hold values from -16 to 16
- prefix_values: bfloat16 [8192, 3072], P('req', 'pre'), may hold values from -6 to 6
- segment_ids: int32 [64, 256], P('req'), may hold values from 0 to 7, never falling along the last dimension, each value on 1 to 64 neighbouring positions
- live_rows: int32 [64], P('req'), may hold values from 64 to 256, as said below
Outputs:
- attended: bfloat16 [16384, 3072], P('req', 'pre')
- suffix_keys: bfloat16 [16384, 3072], P('req', 'pre')
Inputs may be any that keep to these rules, and one draw needn't show every extreme that they name: `live_rows`: every group has at least 64 live rows; some group has all 256 rows live in every draw. `segment_ids`: in each group the request numbers never fall along the rows; a request has at most 64 rows.
All inputs are finite; a program needn't handle non-finite values.
Results may differ from a plain program's by a relative error of at most 0.011.
Values may be sent and summed in bfloat16 or wider, within the bound.
A program may use at most 128 MiB of HBM per device.

v0:
```python
import math

import jax
import jax.numpy as jnp
from jax import lax
from jax.sharding import PartitionSpec as P

HD = 128


epsilon = 1e-06
rope_base = 500000.0
floor_value = -1e30


def rotate(vectors, position):
    half_dim = vectors.shape[-1] // 2
    inverse = jnp.exp(
        -math.log(rope_base) * 2.0 * jnp.arange(half_dim, dtype=jnp.float32) / vectors.shape[-1]
    )
    angles = position.astype(jnp.float32)[:, None] * inverse[None, :]
    cosine = jnp.cos(angles)[:, None, :]
    sine_part = jnp.sin(angles)[:, None, :]
    first_half = vectors[..., :half_dim]
    second_half = vectors[..., half_dim:]
    return jnp.concatenate(
        [
            first_half * cosine - second_half * sine_part,
            second_half * cosine + first_half * sine_part,
        ],
        axis=-1,
    )


def positions(segment, prefix_len):
    row_index = jnp.arange(segment.shape[0], dtype=jnp.int32)
    first_row = jnp.sum((segment[None, :] < segment[:, None]).astype(jnp.int32), axis=1)
    return prefix_len + row_index - first_row


def block_parts(queries_bf, key_rows, value_rows, blocks, scaling):
    head_count = queries_bf.shape[1]
    row_count = queries_bf.shape[0]
    block_len = key_rows.shape[0] // blocks
    scores = (
        jnp.einsum("qhd,khd->hqk", queries_bf, key_rows, preferred_element_type=jnp.float32)
        * scaling
    )
    scores = scores.reshape(head_count, row_count, blocks, block_len)
    block_max = jnp.max(scores, axis=-1)
    weights = jnp.exp(scores - block_max[..., None])
    block_sum = jnp.sum(weights, axis=-1)
    weights_bf = weights.astype(jnp.bfloat16)
    grouped = value_rows.reshape(blocks, block_len, head_count, value_rows.shape[-1])
    summed = jnp.einsum("hqbk,bkhd->hbqd", weights_bf, grouped, preferred_element_type=jnp.float32)
    block_sum = jnp.transpose(block_sum, (0, 2, 1))
    block_out = (summed / block_sum[..., None]).astype(jnp.bfloat16)
    return (jnp.transpose(block_max, (0, 2, 1)), block_sum, block_out)


def absorb(running, block_max, block_sum, block_out):
    best, denominator, numerator = running
    new_best = jnp.maximum(best, jnp.max(block_max, axis=1))
    keep_old = jnp.exp(best - new_best)
    factor = block_sum * jnp.exp(block_max - new_best[:, None, :])
    denominator = denominator * keep_old + jnp.sum(factor, axis=1)
    numerator = numerator * keep_old[..., None] + jnp.sum(
        factor[..., None] * block_out.astype(jnp.float32), axis=1
    )
    return (new_best, denominator, numerator)


def per_device(
    queries_raw,
    keys_raw,
    values,
    query_gain,
    key_gain,
    prefix_keys,
    prefix_values,
    segment_ids,
    live_rows,
):
    row_count, local_width = queries_raw.shape
    head_count = local_width // HD
    query_f = queries_raw.astype(jnp.float32)
    key_f = keys_raw.astype(jnp.float32)
    square_q, square_k = lax.psum(
        (jnp.sum(query_f * query_f, axis=1), jnp.sum(key_f * key_f, axis=1)), "pre"
    )
    full_width = local_width * lax.axis_size("pre")
    normed_q = query_f * lax.rsqrt(square_q / full_width + epsilon)[:, None] * query_gain[None, :]
    normed_k = key_f * lax.rsqrt(square_k / full_width + epsilon)[:, None] * key_gain[None, :]
    shard_rows = prefix_keys.shape[0]
    prefix_len = shard_rows * lax.axis_size("req")
    segment = segment_ids[0]
    live_count = live_rows[0]
    position = positions(segment, prefix_len)
    queries_bf = rotate(normed_q.reshape(row_count, head_count, HD), position).astype(jnp.bfloat16)
    rotated_k = rotate(normed_k.reshape(row_count, head_count, HD), position).astype(jnp.bfloat16)
    row_index = jnp.arange(row_count, dtype=jnp.int32)
    alive = row_index < live_count
    suffix_cache = jnp.where(alive[:, None, None], rotated_k, jnp.zeros_like(rotated_k))
    values_grid = values.reshape(row_count, head_count, HD)
    scaling = 1.0 / math.sqrt(HD)
    lead = ()
    running = (
        jnp.full(lead + (head_count, row_count), floor_value, jnp.float32),
        jnp.zeros(lead + (head_count, row_count), jnp.float32),
        jnp.zeros(lead + (head_count, row_count, HD), jnp.float32),
    )
    carry = running
    key_rows = lax.all_gather(prefix_keys, "req", axis=0, tiled=True)
    value_rows = lax.all_gather(prefix_values, "req", axis=0, tiled=True)
    blocks = key_rows.shape[0] // shard_rows
    group = math.gcd(blocks, max(1, 1024 // shard_rows))
    rounds = blocks // group
    key_grid = key_rows.reshape(rounds, group * shard_rows, head_count, HD)
    value_grid = value_rows.reshape(rounds, group * shard_rows, head_count, HD)

    def advance(inner, pair):
        parts = block_parts(queries_bf, pair[0], pair[1], group, scaling)
        return (absorb(inner, parts[0], parts[1], parts[2]), None)

    carry, unused = lax.scan(advance, carry, (key_grid, value_grid))
    running = carry
    scores = (
        jnp.einsum("qhd,khd->hqk", queries_bf, suffix_cache, preferred_element_type=jnp.float32)
        * scaling
    )
    allowed = (
        (segment[None, :] == segment[:, None])
        & (row_index[None, :] <= row_index[:, None])
        & alive[None, :]
    )
    row_best = jnp.max(jnp.where(allowed[None], scores, floor_value), axis=-1)
    weights = jnp.exp(jnp.where(allowed[None], scores - row_best[..., None], floor_value))
    row_sum = jnp.sum(weights, axis=-1)
    summed = jnp.einsum(
        "hqk,khd->hqd",
        weights.astype(jnp.bfloat16),
        values_grid,
        preferred_element_type=jnp.float32,
    )
    suffix_out = (summed / jnp.maximum(row_sum, 1.0)[..., None]).astype(jnp.bfloat16)
    own_max = row_best[:, None, :]
    own_sum = row_sum[:, None, :]
    own_out = suffix_out[:, None]
    running = absorb(running, own_max, own_sum, own_out)
    best, denominator, numerator = running
    merged = numerator / denominator[..., None]
    merged = jnp.transpose(merged, (1, 0, 2)).reshape(row_count, local_width)
    attended = jnp.where(alive[:, None], merged, 0.0).astype(jnp.bfloat16)
    return (attended, suffix_cache.reshape(row_count, local_width))


def solution(mesh):
    placed = (
        P("req", "pre"),
        P("req", "pre"),
        P("req", "pre"),
        P("pre"),
        P("pre"),
        P("req", "pre"),
        P("req", "pre"),
        P("req", None),
        P("req"),
    )
    return jax.shard_map(
        per_device,
        mesh=mesh,
        in_specs=placed,
        out_specs=(P("req", "pre"), P("req", "pre")),
        check_vma=False,
    )
```

profile of v0, /device:TPU:1, one launch (start us, length us, event | category | flops | bytes accessed | tf_op | source)
XLA Modules:
  0.0 356.4 jit_solution(16673075488465951549)
XLA Ops:
  8.7 1.1 copy.18
  9.8 1.1 copy.24
  11.0 14.7 %all-reduce = (f32[256]{0:T(256)S(1)}, f32[256]{0:T(256)S(1)}) all-reduce(f32[256]{0:T(256)S(1)} %fusion.20, f32[256]{0:T(256)S(1)} %fusion.22), channel_id=1, replica_groups=mesh['req'=64,'pre'=8] {'pre'}, use_global_device_ids=true, to_apply=%region_1.0 | all-reduce | flops 512 | bytes 4096 | tf_op jit(solution)/shard_map/psum | solution.py:88
  25.7 0.8 fusion.21
  28.1 0.8 copy.28
  29.8 0.8 copy.30
  30.8 0.8 pad_maximum_fusion
  31.7 1.3 select_reduce_fusion
  33.0 0.9 copy-done.1
  34.7 69.1 %all-gather.3.cloned.1.call-done = bf16[8192,384]{1,0:T(8,128)(2,1)} async-done(((bf16[128,384]{1,0:T(8,128)(2,1)}), bf16[8192,384]{1,0:T(8,128)(2,1)}) %all-gather.3.cloned.1.call-update) | async-done | bytes 6291472 | tf_op jit(solution)/shard_map/all_gather | solution.py:113
  103.8 16.6 %reshape.200 = bf16[8,1024,3,128]{3,2,1,0:T(4,128)(2,1)} reshape(bf16[8192,384]{1,0:T(8,128)(2,1)} %all-gather.3.cloned.1.call-done) | data formatting | bytes 12582912 | tf_op jit(solution)/shard_map/reshape | solution.py:118
  120.4 7.7 %copy.22 = bf16[8,1024,3,128]{3,1,2,0:T(8,128)(2,1)} copy(bf16[8,1024,3,128]{3,2,1,0:T(4,128)(2,1)} %reshape.200) | data formatting | bytes 12582912
  128.1 62.1 %all-gather.5.cloned.1.call-done = bf16[8192,384]{1,0:T(8,128)(2,1)} async-done(((bf16[128,384]{1,0:T(8,128)(2,1)}), bf16[8192,384]{1,0:T(8,128)(2,1)}) %all-gather.5.cloned.1.call-update) | async-done | bytes 6291472 | tf_op jit(solution)/shard_map/all_gather | solution.py:114
  190.3 16.6 %reshape.201 = bf16[8,1024,3,128]{3,2,1,0:T(4,128)(2,1)} reshape(bf16[8192,384]{1,0:T(8,128)(2,1)} %all-gather.5.cloned.1.call-done) | data formatting | bytes 12582912 | tf_op jit(solution)/shard_map/reshape | solution.py:119
  206.9 7.6 %copy.23 = bf16[8,1024,3,128]{3,1,2,0:T(8,128)(2,1)} copy(bf16[8,1024,3,128]{3,2,1,0:T(4,128)(2,1)} %reshape.201) | data formatting | bytes 12582912
  214.5 130.9 %while.15 = (s32[]{:T(128)}, f32[3,256]{1,0:T(4,128)S(1)}, f32[3,256]{1,0:T(4,128)S(1)}, f32[3,256,128]{2,1,0:T(8,128)S(1)}, bf16[8,1024,3,128]{3,1,2,0:T(8,128)...) while((s32[]{:T(128)}, f32[3,256]{1,0:T(4,128)S(1)}, ...), condition=%wide.region_9.10_spmd.clone, body=%wide.region_3.9_spmd.clone.sunk | while | flops 411516672 | bytes 21034632 | solution.py:125
  214.5 4.0 %bitcast_reduce_fusion.4 = (f32[3,256,8]{1,2,0:T(8,128)}, f32[3,1024,256]{2,1,0:T(8,128)}) fusion(bf16[256,3,128]{2,0,1:T(8,128)(2,1)} %get-tuple-element.197, bf16[8,1024,3,128]{3,1,2,0:T(8,128)(2,1)} %get-tuple-element.196, s32[]{:T(128)} %get-tuple-element.183), kind=kOutput, calls=%fused_computation.21.clone.1 | convolution fusion | flops 202893312 | bytes 4153856 | tf_op jit(solution)/shard_map/while/body/eval_jaxpr/qhd,khd->hqk/dot_general | solution.py:46
  218.5 2.4 copy.43
  220.9 3.2 fusion.59
  224.1 0.8 fusion.60
  224.9 1.2 constant_dynamic-slice_fusion.2
  226.1 4.5 %multiply_reduce_fusion.2 = f32[3,256,128]{2,1,0:T(8,128)S(1)} fusion(f32[3,8,256]{2,1,0:T(8,128)S(1)} %get-tuple-element.172, f32[3,8,256]{2,1,0:T(8,128)} %bitcast.57, bf16[8,128,3,128]{3,1,0,2:T(8,128)(2,1)S(1)} %bitcast.56, f32[3,256,8,128]{3,1,2,0:T(8,128)S(1)} %copy.43, f32[3,256,8]{1,2,0:T(8,128)} %get-tuple-element.168), kind=kOutput, calls=%fused_computation.clone.1 | convolution fusion | flops 206733312 | bytes 4399104 | tf_op jit(solution)/shard_map/while/body/eval_jaxpr/hqbk,bkhd->hbqd/dot_general | solution.py:55
  230.8 4.0 %bitcast_reduce_fusion.4 = (f32[3,256,8]{1,2,0:T(8,128)}, f32[3,1024,256]{2,1,0:T(8,128)}) fusion(bf16[256,3,128]{2,0,1:T(8,128)(2,1)} %get-tuple-element.197, bf16[8,1024,3,128]{3,1,2,0:T(8,128)(2,1)} %get-tuple-element.196, s32[]{:T(128)} %get-tuple-element.183), kind=kOutput, calls=%fused_computation.21.clone.1 | convolution fusion | flops 202893312 | bytes 4153856 | tf_op jit(solution)/shard_map/while/body/eval_jaxpr/qhd,khd->hqk/dot_general | solution.py:46
  234.8 2.4 copy.43
  237.2 3.2 fusion.59
  240.4 0.8 fusion.60
  241.2 1.2 constant_dynamic-slice_fusion.2
  242.4 4.5 %multiply_reduce_fusion.2 = f32[3,256,128]{2,1,0:T(8,128)S(1)} fusion(f32[3,8,256]{2,1,0:T(8,128)S(1)} %get-tuple-element.172, f32[3,8,256]{2,1,0:T(8,128)} %bitcast.57, bf16[8,128,3,128]{3,1,0,2:T(8,128)(2,1)S(1)} %bitcast.56, f32[3,256,8,128]{3,1,2,0:T(8,128)S(1)} %copy.43, f32[3,256,8]{1,2,0:T(8,128)} %get-tuple-element.168), kind=kOutput, calls=%fused_computation.clone.1 | convolution fusion | flops 206733312 | bytes 4399104 | tf_op jit(solution)/shard_map/while/body/eval_jaxpr/hqbk,bkhd->hbqd/dot_general | solution.py:55
  247.2 4.0 %bitcast_reduce_fusion.4 = (f32[3,256,8]{1,2,0:T(8,128)}, f32[3,1024,256]{2,1,0:T(8,128)}) fusion(bf16[256,3,128]{2,0,1:T(8,128)(2,1)} %get-tuple-element.197, bf16[8,1024,3,128]{3,1,2,0:T(8,128)(2,1)} %get-tuple-element.196, s32[]{:T(128)} %get-tuple-element.183), kind=kOutput, calls=%fused_computation.21.clone.1 | convolution fusion | flops 202893312 | bytes 4153856 | tf_op jit(solution)/shard_map/while/body/eval_jaxpr/qhd,khd->hqk/dot_general | solution.py:46
  251.2 2.4 copy.43
  253.6 3.2 fusion.59
  256.8 0.8 fusion.60
  257.6 1.2 constant_dynamic-slice_fusion.2
  258.8 4.5 %multiply_reduce_fusion.2 = f32[3,256,128]{2,1,0:T(8,128)S(1)} fusion(f32[3,8,256]{2,1,0:T(8,128)S(1)} %get-tuple-element.172, f32[3,8,256]{2,1,0:T(8,128)} %bitcast.57, bf16[8,128,3,128]{3,1,0,2:T(8,128)(2,1)S(1)} %bitcast.56, f32[3,256,8,128]{3,1,2,0:T(8,128)S(1)} %copy.43, f32[3,256,8]{1,2,0:T(8,128)} %get-tuple-element.168), kind=kOutput, calls=%fused_computation.clone.1 | convolution fusion | flops 206733312 | bytes 4399104 | tf_op jit(solution)/shard_map/while/body/eval_jaxpr/hqbk,bkhd->hbqd/dot_general | solution.py:55
  263.6 4.0 %bitcast_reduce_fusion.4 = (f32[3,256,8]{1,2,0:T(8,128)}, f32[3,1024,256]{2,1,0:T(8,128)}) fusion(bf16[256,3,128]{2,0,1:T(8,128)(2,1)} %get-tuple-element.197, bf16[8,1024,3,128]{3,1,2,0:T(8,128)(2,1)} %get-tuple-element.196, s32[]{:T(128)} %get-tuple-element.183), kind=kOutput, calls=%fused_computation.21.clone.1 | convolution fusion | flops 202893312 | bytes 4153856 | tf_op jit(solution)/shard_map/while/body/eval_jaxpr/qhd,khd->hqk/dot_general | solution.py:46
  267.6 2.4 copy.43
  270.0 3.2 fusion.59
  273.2 0.8 fusion.60
  274.0 1.2 constant_dynamic-slice_fusion.2
  275.2 4.5 %multiply_reduce_fusion.2 = f32[3,256,128]{2,1,0:T(8,128)S(1)} fusion(f32[3,8,256]{2,1,0:T(8,128)S(1)} %get-tuple-element.172, f32[3,8,256]{2,1,0:T(8,128)} %bitcast.57, bf16[8,128,3,128]{3,1,0,2:T(8,128)(2,1)S(1)} %bitcast.56, f32[3,256,8,128]{3,1,2,0:T(8,128)S(1)} %copy.43, f32[3,256,8]{1,2,0:T(8,128)} %get-tuple-element.168), kind=kOutput, calls=%fused_computation.clone.1 | convolution fusion | flops 206733312 | bytes 4399104 | tf_op jit(solution)/shard_map/while/body/eval_jaxpr/hqbk,bkhd->hbqd/dot_general | solution.py:55
  279.9 4.0 %bitcast_reduce_fusion.4 = (f32[3,256,8]{1,2,0:T(8,128)}, f32[3,1024,256]{2,1,0:T(8,128)}) fusion(bf16[256,3,128]{2,0,1:T(8,128)(2,1)} %get-tuple-element.197, bf16[8,1024,3,128]{3,1,2,0:T(8,128)(2,1)} %get-tuple-element.196, s32[]{:T(128)} %get-tuple-element.183), kind=kOutput, calls=%fused_computation.21.clone.1 | convolution fusion | flops 202893312 | bytes 4153856 | tf_op jit(solution)/shard_map/while/body/eval_jaxpr/qhd,khd->hqk/dot_general | solution.py:46
  284.0 2.4 copy.43
  286.3 3.2 fusion.59
  290.4 1.2 constant_dynamic-slice_fusion.2
  291.5 4.5 %multiply_reduce_fusion.2 = f32[3,256,128]{2,1,0:T(8,128)S(1)} fusion(f32[3,8,256]{2,1,0:T(8,128)S(1)} %get-tuple-element.172, f32[3,8,256]{2,1,0:T(8,128)} %bitcast.57, bf16[8,128,3,128]{3,1,0,2:T(8,128)(2,1)S(1)} %bitcast.56, f32[3,256,8,128]{3,1,2,0:T(8,128)S(1)} %copy.43, f32[3,256,8]{1,2,0:T(8,128)} %get-tuple-element.168), kind=kOutput, calls=%fused_computation.clone.1 | convolution fusion | flops 206733312 | bytes 4399104 | tf_op jit(solution)/shard_map/while/body/eval_jaxpr/hqbk,bkhd->hbqd/dot_general | solution.py:55
  296.3 4.0 %bitcast_reduce_fusion.4 = (f32[3,256,8]{1,2,0:T(8,128)}, f32[3,1024,256]{2,1,0:T(8,128)}) fusion(bf16[256,3,128]{2,0,1:T(8,128)(2,1)} %get-tuple-element.197, bf16[8,1024,3,128]{3,1,2,0:T(8,128)(2,1)} %get-tuple-element.196, s32[]{:T(128)} %get-tuple-element.183), kind=kOutput, calls=%fused_computation.21.clone.1 | convolution fusion | flops 202893312 | bytes 4153856 | tf_op jit(solution)/shard_map/while/body/eval_jaxpr/qhd,khd->hqk/dot_general | solution.py:46
  300.3 2.4 copy.43
  302.7 3.2 fusion.59
  306.7 1.2 constant_dynamic-slice_fusion.2
  307.9 4.5 %multiply_reduce_fusion.2 = f32[3,256,128]{2,1,0:T(8,128)S(1)} fusion(f32[3,8,256]{2,1,0:T(8,128)S(1)} %get-tuple-element.172, f32[3,8,256]{2,1,0:T(8,128)} %bitcast.57, bf16[8,128,3,128]{3,1,0,2:T(8,128)(2,1)S(1)} %bitcast.56, f32[3,256,8,128]{3,1,2,0:T(8,128)S(1)} %copy.43, f32[3,256,8]{1,2,0:T(8,128)} %get-tuple-element.168), kind=kOutput, calls=%fused_computation.clone.1 | convolution fusion | flops 206733312 | bytes 4399104 | tf_op jit(solution)/shard_map/while/body/eval_jaxpr/hqbk,bkhd->hbqd/dot_general | solution.py:55
  312.7 4.0 %bitcast_reduce_fusion.4 = (f32[3,256,8]{1,2,0:T(8,128)}, f32[3,1024,256]{2,1,0:T(8,128)}) fusion(bf16[256,3,128]{2,0,1:T(8,128)(2,1)} %get-tuple-element.197, bf16[8,1024,3,128]{3,1,2,0:T(8,128)(2,1)} %get-tuple-element.196, s32[]{:T(128)} %get-tuple-element.183), kind=kOutput, calls=%fused_computation.21.clone.1 | convolution fusion | flops 202893312 | bytes 4153856 | tf_op jit(solution)/shard_map/while/body/eval_jaxpr/qhd,khd->hqk/dot_general | solution.py:46
  316.7 2.4 copy.43
  319.1 3.2 fusion.59
  322.3 0.8 fusion.60
  323.1 1.2 constant_dynamic-slice_fusion.2
  324.3 4.5 %multiply_reduce_fusion.2 = f32[3,256,128]{2,1,0:T(8,128)S(1)} fusion(f32[3,8,256]{2,1,0:T(8,128)S(1)} %get-tuple-element.172, f32[3,8,256]{2,1,0:T(8,128)} %bitcast.57, bf16[8,128,3,128]{3,1,0,2:T(8,128)(2,1)S(1)} %bitcast.56, f32[3,256,8,128]{3,1,2,0:T(8,128)S(1)} %copy.43, f32[3,256,8]{1,2,0:T(8,128)} %get-tuple-element.168), kind=kOutput, calls=%fused_computation.clone.1 | convolution fusion | flops 206733312 | bytes 4399104 | tf_op jit(solution)/shard_map/while/body/eval_jaxpr/hqbk,bkhd->hbqd/dot_general | solution.py:55
  329.1 4.0 %bitcast_reduce_fusion.4 = (f32[3,256,8]{1,2,0:T(8,128)}, f32[3,1024,256]{2,1,0:T(8,128)}) fusion(bf16[256,3,128]{2,0,1:T(8,128)(2,1)} %get-tuple-element.197, bf16[8,1024,3,128]{3,1,2,0:T(8,128)(2,1)} %get-tuple-element.196, s32[]{:T(128)} %get-tuple-element.183), kind=kOutput, calls=%fused_computation.21.clone.1 | convolution fusion | flops 202893312 | bytes 4153856 | tf_op jit(solution)/shard_map/while/body/eval_jaxpr/qhd,khd->hqk/dot_general | solution.py:46
  333.1 2.4 copy.43
  335.4 3.2 fusion.59
  339.5 1.2 constant_dynamic-slice_fusion.2
  340.7 4.5 %multiply_reduce_fusion.2 = f32[3,256,128]{2,1,0:T(8,128)S(1)} fusion(f32[3,8,256]{2,1,0:T(8,128)S(1)} %get-tuple-element.172, f32[3,8,256]{2,1,0:T(8,128)} %bitcast.57, bf16[8,128,3,128]{3,1,0,2:T(8,128)(2,1)S(1)} %bitcast.56, f32[3,256,8,128]{3,1,2,0:T(8,128)S(1)} %copy.43, f32[3,256,8]{1,2,0:T(8,128)} %get-tuple-element.168), kind=kOutput, calls=%fused_computation.clone.1 | convolution fusion | flops 206733312 | bytes 4399104 | tf_op jit(solution)/shard_map/while/body/eval_jaxpr/hqbk,bkhd->hbqd/dot_general | solution.py:55
  346.3 1.5 fusion.17
  347.9 0.8 copy.31
  348.7 0.8 copy.32
  (104 shorter events, 9.9 us)
Async XLA Ops:
  7.2 19.7 %copy-start.6 = (f32[384]{0:T(512)S(1)}, f32[384]{0:T(512)}, u32[]{:S(2)}) copy-start(f32[384]{0:T(512)} %param.15) | copy-start | bytes 4612
  7.2 96.6 %all-gather.3.cloned.1.call-start = ((), (), s32[]{:S(2)}) async-start(), calls=%async_computation | async-start | bytes 6389760 | tf_op jit(solution)/shard_map/all_gather | solution.py:113
  7.9 182.4 %all-gather.5.cloned.1.call-start = ((), (), s32[]{:S(2)}) async-start(), calls=%async_computation.1 | async-start | bytes 6389760 | tf_op jit(solution)/shard_map/all_gather | solution.py:114
  8.7 19.4 %copy-start.4 = (bf16[256,384]{1,0:T(8,128)(2,1)S(1)}, bf16[256,384]{1,0:T(8,128)(2,1)}, u32[]{:S(2)}) copy-start(bf16[256,384]{1,0:T(8,128)(2,1)} %param.13) | copy-start | bytes 589828
  9.8 19.1 %copy-start.5 = (s32[1,256]{1,0:T(1,128)S(1)}, s32[1,256]{1,0:T(1,128)}, u32[]{:S(2)}) copy-start(s32[1,256]{1,0:T(1,128)} %param.18) | copy-start | bytes 3076
  30.7 89.8 %copy-start.7 = (pred[256]{0:T(512)(128)(4,1)}, pred[256]{0:T(512)(128)(4,1)S(1)}, u32[]{:S(2)}) copy-start(pred[256]{0:T(512)(128)(4,1)S(1)} %iota_compare_fusion.1) | copy-start | bytes 772
  31.7 88.7 %copy-start.3 = (pred[256,256]{0,1:T(8,128)(4,1)}, pred[256,256]{0,1:T(8,128)(4,1)S(1)}, u32[]{:S(2)}) copy-start(pred[256,256]{0,1:T(8,128)(4,1)S(1)} %fusion.30) | copy-start | bytes 196612
  33.0 0.9 copy-start.1
  220.8 3.2 copy-start
  237.2 3.2 copy-start
  253.6 3.2 copy-start
  270.0 3.2 copy-start
  286.3 3.2 copy-start
  302.7 3.2 copy-start
  319.1 3.2 copy-start
  335.4 3.2 copy-start
  345.4 2.4 copy-start.2
  345.4 2.4 copy-start.8
Sparse Core Ops, SparseCore 0:
  11.3 92.4 all-gather.2
  107.1 83.1 all-gather.4
where the time goes:
time: 360 us; the launch traced here: 356 us
  waiting for transfers between devices  133 us (37%)
  local copies, waits for them, and re-layouts  84.4 us (23%)
  matrix products  70.8 us (20%)
  other arithmetic  38.4 us (11%)
  between operations  14.9 us (4%)
  blocking collectives  14.7 us (4%)
    all_gather x1, waiting for transfers between devices, per_device(): key_rows = lax.all_gather(prefix_keys, 'req', axis=0, tiled=True)  69.1 us
    all_gather x1, waiting for transfers between devices, per_device(): value_rows = lax.all_gather(prefix_values, 'req', axis=0, tiled=True)  62.1 us
    dot_general x8, matrix products, block_parts(): jnp.einsum('hqbk,bkhd->hbqd', weights_bf, grouped, preferred_element_type...  36 us
    dot_general x8, matrix products, block_parts(): jnp.einsum('qhd,khd->hqk', queries_bf, key_rows, preferred_element_type=j...  32 us
    reduce_sum x8, other arithmetic, block_parts(): block_sum = jnp.sum(weights, axis=-1)  25.5 us
    unnamed x27, local copies, waits for them, and re-layouts  21.5 us
    reshape x8, local copies, waits for them, and re-layouts, block_parts(): scores = scores.reshape(head_count, row_count, blocks, block_len)  19 us
    reshape x1, local copies, waits for them, and re-layouts, per_device(): key_grid = key_rows.reshape(rounds, group * shard_rows, head_count, HD)  16.6 us
  transfers between devices with their start and end apart: 2, of which 2 were waited for; matrix products, arithmetic and copies ran while one was open for 10% of the time, Pallas kernels for 0%

commit v1 on v0

v1 whole, which is shorter than its diff:
```python
import math

import jax
import jax.numpy as jnp
from jax import lax
from jax.experimental import pallas as pl
from jax.experimental.pallas import tpu as pltpu
from jax.sharding import PartitionSpec as P

HD = 128
KV_BLOCK = 2048


epsilon = 1e-06
rope_base = 500000.0
floor_value = -1e30


def rotate(vectors, position):
    half_dim = vectors.shape[-1] // 2
    inverse = jnp.exp(
        -math.log(rope_base) * 2.0 * jnp.arange(half_dim, dtype=jnp.float32) / vectors.shape[-1]
    )
    angles = position.astype(jnp.float32)[:, None] * inverse[None, :]
    cosine = jnp.cos(angles)[:, None, :]
    sine_part = jnp.sin(angles)[:, None, :]
    first_half = vectors[..., :half_dim]
    second_half = vectors[..., half_dim:]
    return jnp.concatenate(
        [
            first_half * cosine - second_half * sine_part,
            second_half * cosine + first_half * sine_part,
        ],
        axis=-1,
    )


def positions(segment, prefix_len):
    row_index = jnp.arange(segment.shape[0], dtype=jnp.int32)
    first_row = jnp.sum((segment[None, :] < segment[:, None]).astype(jnp.int32), axis=1)
    return prefix_len + row_index - first_row


def flash_kernel(
    q_ref, k_ref, v_ref, oo_ref, om_ref, os_ref, alive_ref, out_ref, m_sc, l_sc, acc_sc, *, scaling
):
    j = pl.program_id(1)

    @pl.when(j == 0)
    def _():
        m_sc[...] = jnp.full(m_sc.shape, floor_value, jnp.float32)
        l_sc[...] = jnp.zeros(l_sc.shape, jnp.float32)
        acc_sc[...] = jnp.zeros(acc_sc.shape, jnp.float32)

    s = (
        lax.dot_general(
            q_ref[...],
            k_ref[...],
            (((1,), (1,)), ((), ())),
            preferred_element_type=jnp.float32,
        )
        * scaling
    )
    m_prev = m_sc[...]
    m_new = jnp.maximum(m_prev, jnp.max(s, axis=1, keepdims=True))
    alpha = jnp.exp(m_prev - m_new)
    p = jnp.exp(s - m_new)
    l_sc[...] = alpha * l_sc[...] + jnp.sum(p, axis=1, keepdims=True)
    acc_sc[...] = alpha * acc_sc[...] + jnp.dot(
        p.astype(jnp.bfloat16), v_ref[...], preferred_element_type=jnp.float32
    )
    m_sc[...] = m_new

    @pl.when(j == pl.num_programs(1) - 1)
    def _():
        m = m_sc[...]
        own_max = om_ref[...]
        best = jnp.maximum(m, own_max)
        prefix_weight = jnp.exp(m - best)
        own_weight = os_ref[...] * jnp.exp(own_max - best)
        numerator = acc_sc[...] * prefix_weight + own_weight * oo_ref[...].astype(jnp.float32)
        denominator = l_sc[...] * prefix_weight + own_weight
        merged = numerator / denominator
        out_ref[...] = jnp.where(alive_ref[...] > 0.0, merged, 0.0).astype(out_ref.dtype)


def prefix_attention(queries2d, kv_rows, own_out2d, own_max, own_sum, alive_f, head_count, scaling):
    row_count = queries2d.shape[0]
    total = kv_rows.shape[0]
    block = min(KV_BLOCK, total)
    steps = total // block
    kernel = lambda *refs: flash_kernel(*refs, scaling=scaling)
    return pl.pallas_call(
        kernel,
        grid=(head_count, steps),
        in_specs=[
            pl.BlockSpec((row_count, HD), lambda h, j: (0, h)),
            pl.BlockSpec((block, HD), lambda h, j: (j, h)),
            pl.BlockSpec((block, HD), lambda h, j: (j, head_count + h)),
            pl.BlockSpec((row_count, HD), lambda h, j: (0, h)),
            pl.BlockSpec((None, row_count, 1), lambda h, j: (h, 0, 0)),
            pl.BlockSpec((None, row_count, 1), lambda h, j: (h, 0, 0)),
            pl.BlockSpec((row_count, 1), lambda h, j: (0, 0)),
        ],
        out_specs=pl.BlockSpec((row_count, HD), lambda h, j: (0, h)),
        out_shape=jax.ShapeDtypeStruct((row_count, head_count * HD), jnp.bfloat16),
        scratch_shapes=[
            pltpu.VMEM((row_count, 1), jnp.float32),
            pltpu.VMEM((row_count, 1), jnp.float32),
            pltpu.VMEM((row_count, HD), jnp.float32),
        ],
        compiler_params=pltpu.CompilerParams(dimension_semantics=("arbitrary", "arbitrary")),
    )(queries2d, kv_rows, kv_rows, own_out2d, own_max, own_sum, alive_f)


def per_device(
    queries_raw,
    keys_raw,
    values,
    query_gain,
    key_gain,
    prefix_keys,
    prefix_values,
    segment_ids,
    live_rows,
):
    row_count, local_width = queries_raw.shape
    head_count = local_width // HD
    kv_block = jnp.concatenate([prefix_keys, prefix_values], axis=1)
    kv_rows = lax.all_gather(kv_block, "req", axis=0, tiled=True)
    query_f = queries_raw.astype(jnp.float32)
    key_f = keys_raw.astype(jnp.float32)
    square_q, square_k = lax.psum(
        (jnp.sum(query_f * query_f, axis=1), jnp.sum(key_f * key_f, axis=1)), "pre"
    )
    full_width = local_width * lax.axis_size("pre")
    normed_q = query_f * lax.rsqrt(square_q / full_width + epsilon)[:, None] * query_gain[None, :]
    normed_k = key_f * lax.rsqrt(square_k / full_width + epsilon)[:, None] * key_gain[None, :]
    shard_rows = prefix_keys.shape[0]
    prefix_len = shard_rows * lax.axis_size("req")
    segment = segment_ids[0]
    live_count = live_rows[0]
    position = positions(segment, prefix_len)
    queries_bf = rotate(normed_q.reshape(row_count, head_count, HD), position).astype(jnp.bfloat16)
    rotated_k = rotate(normed_k.reshape(row_count, head_count, HD), position).astype(jnp.bfloat16)
    row_index = jnp.arange(row_count, dtype=jnp.int32)
    alive = row_index < live_count
    suffix_cache = jnp.where(alive[:, None, None], rotated_k, jnp.zeros_like(rotated_k))
    values_grid = values.reshape(row_count, head_count, HD)
    scaling = 1.0 / math.sqrt(HD)
    scores = (
        jnp.einsum("qhd,khd->hqk", queries_bf, suffix_cache, preferred_element_type=jnp.float32)
        * scaling
    )
    allowed = (
        (segment[None, :] == segment[:, None])
        & (row_index[None, :] <= row_index[:, None])
        & alive[None, :]
    )
    row_best = jnp.max(jnp.where(allowed[None], scores, floor_value), axis=-1)
    weights = jnp.exp(jnp.where(allowed[None], scores - row_best[..., None], floor_value))
    row_sum = jnp.sum(weights, axis=-1)
    summed = jnp.einsum(
        "hqk,khd->qhd",
        weights.astype(jnp.bfloat16),
        values_grid,
        preferred_element_type=jnp.float32,
    )
    suffix_out = (summed / jnp.maximum(row_sum, 1.0).T[:, :, None]).astype(jnp.bfloat16)
    attended = prefix_attention(
        queries_bf.reshape(row_count, local_width),
        kv_rows,
        suffix_out.reshape(row_count, local_width),
        row_best[:, :, None],
        row_sum[:, :, None],
        alive.astype(jnp.float32)[:, None],
        head_count,
        scaling,
    )
    return (attended, suffix_cache.reshape(row_count, local_width))


def solution(mesh):
    placed = (
        P("req", "pre"),
        P("req", "pre"),
        P("req", "pre"),
        P("pre"),
        P("pre"),
        P("req", "pre"),
        P("req", "pre"),
        P("req", None),
        P("req"),
    )
    return jax.shard_map(
        per_device,
        mesh=mesh,
        in_specs=placed,
        out_specs=(P("req", "pre"), P("req", "pre")),
        check_vma=False,
    )
```

time: 360 us -> 139 us (0.39); the launches traced: 356 us -> 139 us
  local copies, waits for them, and re-layouts: 84.4 us -> 8.61 us
  matrix products: 70.8 us -> 0.64 us
  waiting for transfers between devices: 133 us -> 75.1 us
  other arithmetic: 38.4 us -> 6.31 us
  Pallas kernels: 0 us -> 19 us
    dot_general x17 -> x1, matrix products: 69.5 us -> 0.31 us  [per_device(): jnp.einsum('hqk,khd->qhd', weights.astype(jnp.bfloat16), values_grid, pre...]
    all_gather x2 -> x1, waiting for transfers between devices: 131 us -> 75.1 us  [per_device(): kv_rows = lax.all_gather(kv_block, 'req', axis=0, tiled=True)]
    reshape x10 -> x1, local copies, waits for them, and re-layouts: 52.2 us -> 0.82 us  [per_device(): suffix_out.reshape(row_count, local_width)]
    reduce_sum x16 -> x0, other arithmetic: 31.7 us -> none  [the longest x8 25.5 us: block_parts(): block_sum = jnp.sum(weights, axis=-1)]
    pallas_call x0 -> x1, Pallas kernels: none -> 19 us  [prefix_attention(): pl.pallas_call(kernel, grid=(head_count, steps), in_specs=[pl.BlockSpec((...]
    unnamed x27 -> x10, local copies, waits for them, and re-layouts: 21.5 us -> 4.68 us
    dynamic_slice x8 -> x0, local copies, waits for them, and re-layouts: 9.53 us -> none  [per_device(): carry, unused = lax.scan(advance, carry, (key_grid, value_grid))]
  transfers between devices with their start and end apart: 2 -> 1, of which waited for: 2 -> 1; matrix products, arithmetic and copies ran while one was open for 10% -> 10% of each run, Pallas kernels for 0% -> 0%
where the time goes in v1:
time: 139 us
  waiting for transfers between devices  75.1 us (54%)
  Pallas kernels  19 us (14%)
  between operations  14.8 us (11%)
  blocking collectives  14.7 us (11%)
  local copies, waits for them, and re-layouts  8.61 us (6%)
  other arithmetic  6.31 us (5%)
    all_gather x1, waiting for transfers between devices, per_device(): kv_rows = lax.all_gather(kv_block, 'req', axis=0, tiled=True)  75.1 us
    pallas_call x1, Pallas kernels, prefix_attention(): pl.pallas_call(kernel, grid=(head_count, steps), in_specs=[pl.BlockSpec((...  19 us
    psum x1, blocking collectives, per_device(): lax.psum((jnp.sum(query_f * query_f, axis=1), jnp.sum(key_f * key_f, axis...  14.7 us
    unnamed x10, local copies, waits for them, and re-layouts  4.68 us
  transfers between devices with their start and end apart: 1, of which 1 were waited for; matrix products, arithmetic and copies ran while one was open for 10% of the time, Pallas kernels for 0%

profile of v1, /device:TPU:1, one launch (start us, length us, event | category | flops | bytes accessed | tf_op | source)
XLA Modules:
  0.0 139.2 jit_solution(9749306776274703703)
XLA Ops:
  7.2 0.0 copy-start
  7.2 0.0 all-gather.2.cloned.1.call-start
  7.2 1.6 %pad_maximum_fusion = bf16[128,768]{1,0:T(8,128)(2,1)} fusion(bf16[128,384]{1,0:T(8,128)(2,1)} %param.15, bf16[128,384]{1,0:T(8,128)(2,1)} %param.14), kind=kLoop, calls=%fused_computation.29 | loop fusion | flops 393216 | bytes 393216 | tf_op jit(solution)/shard_map/concatenate | solution.py:129
  8.9 0.0 all-gather.2.cloned.1.call-update
  8.9 1.1 copy.19
  9.9 1.1 copy.15
  11.0 0.1 fusion.4
  11.1 0.1 fusion.6
  11.2 14.7 %all-reduce = (f32[256]{0:T(256)S(1)}, f32[256]{0:T(256)S(1)}) all-reduce(f32[256]{0:T(256)S(1)} %fusion.4, f32[256]{0:T(256)S(1)} %fusion.6), channel_id=1, replica_groups=mesh['req'=64,'pre'=8] {'pre'}, use_global_device_ids=true, to_apply=%region_1.0 | all-reduce | flops 512 | bytes 4096 | tf_op jit(solution)/shard_map/psum | solution.py:133
  25.8 0.8 fusion.7
  26.7 0.2 copy.34
  26.9 0.2 copy.33
  27.0 0.8 fusion.5
  27.9 0.2 copy.31
  28.0 0.2 copy.32
  28.2 0.9 convert_reduce_fusion
  29.1 0.5 multiply_cosine_fusion
  29.6 0.2 multiply_subtract_fusion
  29.9 0.1 maximum_convert_fusion
  30.0 0.1 copy.18
  30.2 0.8 copy.24.refs_0_
  31.0 1.1 copy.22
  32.7 0.1 maximum_convert_fusion.1
  32.8 0.1 copy.28
  33.0 0.0 copy-done
  33.0 0.1 fusion.13
  33.1 0.3 select_reduce_fusion
  33.5 0.2 fusion.2
  33.7 0.3 fusion.1
  34.0 0.8 copy.25.refs_3_
  34.8 1.0 copy.26.refs_4_
  35.8 1.0 copy.27.refs_5_
  36.8 0.8 copy.29
  37.6 0.7 fusion.16.refs_6_
  38.2 75.1 %all-gather.2.cloned.1.call-done.refs_1_.refs_2_ = bf16[8192,768]{1,0:T(8,128)(2,1)} async-done(((bf16[128,768]{1,0:T(8,128)(2,1)}), bf16[8192,768]{1,0:T(8,128)(2,1)}) %all-gather.2.cloned.1.call-update) | async-done | bytes 12582928 | tf_op jit(solution)/shard_map/all_gather | solution.py:130
  113.3 19.0 %shard_map.104 = bf16[256,384]{1,0:T(8,128)(2,1)} custom-call(bf16[256,384]{1,0:T(8,128)(2,1)} %copy.24.refs_0_, bf16[8192,768]{1,0:T(8,128)(2,1)} %all-gather.2.cloned.1.call-done.refs_1_.refs_2_, bf16[8192,768]{1,0:T(8,128)(2,1)} %all-gather.2.cloned.1.call-done.refs_1_.refs_2_, bf16[256,384]{1,0:T(8,128)(2,1)} %copy.25.refs_3_, ...), custom_call_target="tpu_custom_call" | custom-call | tf_op jit(solution)/shard_map/pallas_call | solution.py:93
  (8 shorter events, 0.1 us)
Async XLA Ops:
  7.2 25.8 %copy-start = (s32[1,256]{1,0:T(1,128)S(1)}, s32[1,256]{1,0:T(1,128)}, u32[]{:S(2)}) copy-start(s32[1,256]{1,0:T(1,128)} %param.16) | copy-start | bytes 3076
  7.2 106.1 %all-gather.2.cloned.1.call-start = ((), (), s32[]{:S(2)}) async-start(), calls=%async_computation | async-start | bytes 12779520 | tf_op jit(solution)/shard_map/all_gather | solution.py:130
Sparse Core Ops, SparseCore 0:
  11.9 101.3 all-gather.1

commit v2 on v1

--- a/solution.py
+++ b/solution.py
@@ -8,7 +8,7 @@
 from jax.sharding import PartitionSpec as P
 
 HD = 128
-KV_BLOCK = 2048
+KV_BLOCK = 8192
 
 
 epsilon = 1e-06

time: 139 us -> 136 us (0.978)
  Pallas kernels: 19 us -> 16 us
    pallas_call x1, Pallas kernels: 19 us -> 16 us  [prefix_attention(): pl.pallas_call(kernel, grid=(head_count, steps), in_specs=[pl.BlockSpec((...]
where the time goes in v2:
time: 136 us
  waiting for transfers between devices  75.1 us (55%)
  Pallas kernels  16 us (12%)
  between operations  14.8 us (11%)
  blocking collectives  14.7 us (11%)
  local copies, waits for them, and re-layouts  8.61 us (6%)
  other arithmetic  6.31 us (5%)
    all_gather x1, waiting for transfers between devices, per_device(): kv_rows = lax.all_gather(kv_block, 'req', axis=0, tiled=True)  75.1 us
    pallas_call x1, Pallas kernels, prefix_attention(): pl.pallas_call(kernel, grid=(head_count, steps), in_specs=[pl.BlockSpec((...  16 us
    psum x1, blocking collectives, per_device(): lax.psum((jnp.sum(query_f * query_f, axis=1), jnp.sum(key_f * key_f, axis...  14.7 us
    unnamed x10, local copies, waits for them, and re-layouts  4.68 us
  transfers between devices with their start and end apart: 1, of which 1 were waited for; matrix products, arithmetic and copies ran while one was open for 10% of the time, Pallas kernels for 0%

profile of v2, /device:TPU:1, one launch (start us, length us, event | category | flops | bytes accessed | tf_op | source)
XLA Modules:
  0.0 136.2 jit_solution(2105123704891560444)
XLA Ops:
  7.2 0.0 copy-start
  7.2 0.0 all-gather.2.cloned.1.call-start
  7.2 1.6 %pad_maximum_fusion = bf16[128,768]{1,0:T(8,128)(2,1)} fusion(bf16[128,384]{1,0:T(8,128)(2,1)} %param.15, bf16[128,384]{1,0:T(8,128)(2,1)} %param.14), kind=kLoop, calls=%fused_computation.29 | loop fusion | flops 393216 | bytes 393216 | tf_op jit(solution)/shard_map/concatenate | solution.py:129
  8.9 0.0 all-gather.2.cloned.1.call-update
  8.9 1.1 copy.19
  9.9 1.1 copy.15
  11.0 0.1 fusion.4
  11.1 0.1 fusion.6
  11.2 14.7 %all-reduce = (f32[256]{0:T(256)S(1)}, f32[256]{0:T(256)S(1)}) all-reduce(f32[256]{0:T(256)S(1)} %fusion.4, f32[256]{0:T(256)S(1)} %fusion.6), channel_id=1, replica_groups=mesh['req'=64,'pre'=8] {'pre'}, use_global_device_ids=true, to_apply=%region_1.0 | all-reduce | flops 512 | bytes 4096 | tf_op jit(solution)/shard_map/psum | solution.py:133
  25.8 0.8 fusion.7
  26.7 0.2 copy.34
  26.9 0.2 copy.33
  27.0 0.8 fusion.5
  27.9 0.2 copy.31
  28.0 0.2 copy.32
  28.2 0.9 convert_reduce_fusion
  29.1 0.5 multiply_cosine_fusion
  29.6 0.2 multiply_subtract_fusion
  29.9 0.1 maximum_convert_fusion
  30.0 0.1 copy.18
  30.2 0.8 copy.24.refs_0_
  31.0 1.1 copy.22
  32.7 0.1 maximum_convert_fusion.1
  32.8 0.1 copy.28
  33.0 0.0 copy-done
  33.0 0.1 fusion.13
  33.1 0.3 select_reduce_fusion
  33.5 0.2 fusion.2
  33.7 0.3 fusion.1
  34.0 0.8 copy.25.refs_3_
  34.8 1.0 copy.26.refs_4_
  35.8 1.0 copy.27.refs_5_
  36.8 0.8 copy.29
  37.6 0.7 fusion.16.refs_6_
  38.2 75.1 %all-gather.2.cloned.1.call-done.refs_1_.refs_2_ = bf16[8192,768]{1,0:T(8,128)(2,1)} async-done(((bf16[128,768]{1,0:T(8,128)(2,1)}), bf16[8192,768]{1,0:T(8,128)(2,1)}) %all-gather.2.cloned.1.call-update) | async-done | bytes 12582928 | tf_op jit(solution)/shard_map/all_gather | solution.py:130
  113.3 16.0 %shard_map.104 = bf16[256,384]{1,0:T(8,128)(2,1)} custom-call(bf16[256,384]{1,0:T(8,128)(2,1)} %copy.24.refs_0_, bf16[8192,768]{1,0:T(8,128)(2,1)} %all-gather.2.cloned.1.call-done.refs_1_.refs_2_, bf16[8192,768]{1,0:T(8,128)(2,1)} %all-gather.2.cloned.1.call-done.refs_1_.refs_2_, bf16[256,384]{1,0:T(8,128)(2,1)} %copy.25.refs_3_, ...), custom_call_target="tpu_custom_call" | custom-call | tf_op jit(solution)/shard_map/pallas_call | solution.py:93
  (8 shorter events, 0.1 us)
Async XLA Ops:
  7.2 25.8 %copy-start = (s32[1,256]{1,0:T(1,128)S(1)}, s32[1,256]{1,0:T(1,128)}, u32[]{:S(2)}) copy-start(s32[1,256]{1,0:T(1,128)} %param.16) | copy-start | bytes 3076
  7.2 106.1 %all-gather.2.cloned.1.call-start = ((), (), s32[]{:S(2)}) async-start(), calls=%async_computation | async-start | bytes 12779520 | tf_op jit(solution)/shard_map/all_gather | solution.py:130
Sparse Core Ops, SparseCore 0:
  11.9 101.3 all-gather.1

commit v3 on v2

v3 whole, which is shorter than its diff:
```python
import math

import jax
import jax.numpy as jnp
from jax import lax
from jax.experimental import pallas as pl
from jax.experimental.pallas import tpu as pltpu
from jax.sharding import PartitionSpec as P

HD = 128


epsilon = 1e-06
rope_base = 500000.0
floor_value = -1e30


def rotate(vectors, position):
    half_dim = vectors.shape[-1] // 2
    inverse = jnp.exp(
        -math.log(rope_base) * 2.0 * jnp.arange(half_dim, dtype=jnp.float32) / vectors.shape[-1]
    )
    angles = position.astype(jnp.float32)[:, None] * inverse[None, :]
    cosine = jnp.cos(angles)[:, None, :]
    sine_part = jnp.sin(angles)[:, None, :]
    first_half = vectors[..., :half_dim]
    second_half = vectors[..., half_dim:]
    return jnp.concatenate(
        [
            first_half * cosine - second_half * sine_part,
            second_half * cosine + first_half * sine_part,
        ],
        axis=-1,
    )


def positions(segment, prefix_len):
    row_index = jnp.arange(segment.shape[0], dtype=jnp.int32)
    first_row = jnp.sum((segment[None, :] < segment[:, None]).astype(jnp.int32), axis=1)
    return prefix_len + row_index - first_row


def flash_kernel(q_ref, k_ref, v_ref, oo_ref, om_ref, os_ref, alive_ref, out_ref):
    keys = k_ref[...].reshape(-1, HD)
    vals = v_ref[...].reshape(-1, HD)
    s = lax.dot_general(
        q_ref[...],
        keys,
        (((1,), (1,)), ((), ())),
        preferred_element_type=jnp.float32,
    )
    m = jnp.max(s, axis=1, keepdims=True)
    p = jnp.exp(s - m)
    prefix_sum = jnp.sum(p, axis=1, keepdims=True)
    prefix_acc = jnp.dot(p.astype(jnp.bfloat16), vals, preferred_element_type=jnp.float32)
    own_max = om_ref[...]
    best = jnp.maximum(m, own_max)
    prefix_weight = jnp.exp(m - best)
    own_weight = os_ref[...] * jnp.exp(own_max - best)
    numerator = prefix_acc * prefix_weight + own_weight * oo_ref[...].astype(jnp.float32)
    denominator = prefix_sum * prefix_weight + own_weight
    merged = numerator / denominator
    out_ref[...] = jnp.where(alive_ref[...] > 0.0, merged, 0.0).astype(out_ref.dtype)


def prefix_attention(scaled_q2d, kv_rows, own_out2d, own_max, own_sum, alive_f, head_count):
    row_count = scaled_q2d.shape[0]
    owners, _, shard_rows, _ = kv_rows.shape
    return pl.pallas_call(
        flash_kernel,
        grid=(head_count,),
        in_specs=[
            pl.BlockSpec((row_count, HD), lambda h: (0, h)),
            pl.BlockSpec((owners, None, shard_rows, HD), lambda h: (0, 0, 0, h)),
            pl.BlockSpec((owners, None, shard_rows, HD), lambda h: (0, 1, 0, h)),
            pl.BlockSpec((row_count, HD), lambda h: (0, h)),
            pl.BlockSpec((None, row_count, 1), lambda h: (h, 0, 0)),
            pl.BlockSpec((None, row_count, 1), lambda h: (h, 0, 0)),
            pl.BlockSpec((row_count, 1), lambda h: (0, 0)),
        ],
        out_specs=pl.BlockSpec((row_count, HD), lambda h: (0, h)),
        out_shape=jax.ShapeDtypeStruct((row_count, head_count * HD), jnp.bfloat16),
        compiler_params=pltpu.CompilerParams(dimension_semantics=("arbitrary",)),
    )(scaled_q2d, kv_rows, kv_rows, own_out2d, own_max, own_sum, alive_f)


def per_device(
    queries_raw,
    keys_raw,
    values,
    query_gain,
    key_gain,
    prefix_keys,
    prefix_values,
    segment_ids,
    live_rows,
):
    row_count, local_width = queries_raw.shape
    head_count = local_width // HD
    kv_block = jnp.stack([prefix_keys, prefix_values], axis=0)
    kv_rows = lax.all_gather(kv_block, "req", axis=0)
    query_f = queries_raw.astype(jnp.float32)
    key_f = keys_raw.astype(jnp.float32)
    square_q, square_k = lax.psum(
        (jnp.sum(query_f * query_f, axis=1), jnp.sum(key_f * key_f, axis=1)), "pre"
    )
    full_width = local_width * lax.axis_size("pre")
    normed_q = query_f * lax.rsqrt(square_q / full_width + epsilon)[:, None] * query_gain[None, :]
    normed_k = key_f * lax.rsqrt(square_k / full_width + epsilon)[:, None] * key_gain[None, :]
    shard_rows = prefix_keys.shape[0]
    prefix_len = shard_rows * lax.axis_size("req")
    segment = segment_ids[0]
    live_count = live_rows[0]
    position = positions(segment, prefix_len)
    rotated_q = rotate(normed_q.reshape(row_count, head_count, HD), position)
    queries_bf = rotated_q.astype(jnp.bfloat16)
    rotated_k = rotate(normed_k.reshape(row_count, head_count, HD), position).astype(jnp.bfloat16)
    row_index = jnp.arange(row_count, dtype=jnp.int32)
    alive = row_index < live_count
    suffix_cache = jnp.where(alive[:, None, None], rotated_k, jnp.zeros_like(rotated_k))
    values_grid = values.reshape(row_count, head_count, HD)
    scaling = 1.0 / math.sqrt(HD)
    scores = (
        jnp.einsum("qhd,khd->hqk", queries_bf, suffix_cache, preferred_element_type=jnp.float32)
        * scaling
    )
    allowed = (
        (segment[None, :] == segment[:, None])
        & (row_index[None, :] <= row_index[:, None])
        & alive[None, :]
    )
    row_best = jnp.max(jnp.where(allowed[None], scores, floor_value), axis=-1)
    weights = jnp.exp(jnp.where(allowed[None], scores - row_best[..., None], floor_value))
    row_sum = jnp.sum(weights, axis=-1)
    summed = jnp.einsum(
        "hqk,khd->qhd",
        weights.astype(jnp.bfloat16),
        values_grid,
        preferred_element_type=jnp.float32,
    )
    suffix_out = (summed / jnp.maximum(row_sum, 1.0).T[:, :, None]).astype(jnp.bfloat16)
    scaled_q = (rotated_q * scaling).astype(jnp.bfloat16)
    attended = prefix_attention(
        scaled_q.reshape(row_count, local_width),
        kv_rows,
        suffix_out.reshape(row_count, local_width),
        row_best[:, :, None],
        row_sum[:, :, None],
        alive.astype(jnp.float32)[:, None],
        head_count,
    )
    return (attended, suffix_cache.reshape(row_count, local_width))


def solution(mesh):
    placed = (
        P("req", "pre"),
        P("req", "pre"),
        P("req", "pre"),
        P("pre"),
        P("pre"),
        P("req", "pre"),
        P("req", "pre"),
        P("req", None),
        P("req"),
    )
    return jax.shard_map(
        per_device,
        mesh=mesh,
        in_specs=placed,
        out_specs=(P("req", "pre"), P("req", "pre")),
        check_vma=False,
    )
```

time: 136 us -> 134 us (0.985)
  Pallas kernels: 16 us -> 13.8 us
    pallas_call x1, Pallas kernels: 16 us -> 13.8 us  [prefix_attention(): pl.pallas_call(flash_kernel, grid=(head_count,), in_specs=[pl.BlockSpec((...]
    another operation x0 -> x1, other arithmetic: none -> 1.64 us  [per_device(): kv_block = jnp.stack([prefix_keys, prefix_values], axis=0)]
    concatenate x1 -> x0, other arithmetic: 1.64 us -> none  [per_device(): kv_block = jnp.concatenate([prefix_keys, prefix_values], axis=1)]
    unnamed x10 -> x8, local copies, waits for them, and re-layouts: 4.68 us -> 4.68 us
  transfers between devices with their start and end apart: 1 -> 1, of which waited for: 1 -> 1; matrix products, arithmetic and copies ran while one was open for 10% -> 11% of each run, Pallas kernels for 0% -> 0%
where the time goes in v3:
time: 134 us
  waiting for transfers between devices  74.3 us (55%)
  between operations  14.8 us (11%)
  blocking collectives  14.7 us (11%)
  Pallas kernels  13.8 us (10%)
  local copies, waits for them, and re-layouts  8.6 us (6%)
  other arithmetic  7.09 us (5%)
    all_gather x1, waiting for transfers between devices, per_device(): kv_rows = lax.all_gather(kv_block, 'req', axis=0)  74.3 us
    psum x1, blocking collectives, per_device(): lax.psum((jnp.sum(query_f * query_f, axis=1), jnp.sum(key_f * key_f, axis...  14.7 us
    pallas_call x1, Pallas kernels, prefix_attention(): pl.pallas_call(flash_kernel, grid=(head_count,), in_specs=[pl.BlockSpec((...  13.8 us
    unnamed x8, local copies, waits for them, and re-layouts  4.68 us
  transfers between devices with their start and end apart: 1, of which 1 were waited for; matrix products, arithmetic and copies ran while one was open for 11% of the time, Pallas kernels for 0%

profile of v3, /device:TPU:1, one launch (start us, length us, event | category | flops | bytes accessed | tf_op | source)
XLA Modules:
  0.0 134.1 jit_solution(4204904227906323469)
XLA Ops:
  7.2 0.0 all-gather.3.cloned.1.call-start
  7.2 1.6 %pad_maximum_fusion.1 = bf16[2,128,384]{2,1,0:T(8,128)(2,1)} fusion(bf16[1,128,384]{2,1,0:T(8,128)(2,1)} %bitcast.32, bf16[1,128,384]{2,1,0:T(8,128)(2,1)} %bitcast.33), kind=kLoop, calls=%fused_computation.30 | loop fusion | flops 98304 | bytes 393216 | tf_op jit(solution)/shard_map/stack | solution.py:100
  8.9 0.0 all-gather.3.cloned.1.call-update
  8.9 1.1 copy.30
  9.9 1.1 copy.34
  11.0 0.1 fusion.4
  11.1 0.1 fusion.6
  11.2 14.7 %all-reduce = (f32[256]{0:T(256)S(1)}, f32[256]{0:T(256)S(1)}) all-reduce(f32[256]{0:T(256)S(1)} %fusion.4, f32[256]{0:T(256)S(1)} %fusion.6), channel_id=1, replica_groups=mesh['req'=64,'pre'=8] {'pre'}, use_global_device_ids=true, to_apply=%region_1.0 | all-reduce | flops 512 | bytes 4096 | tf_op jit(solution)/shard_map/psum | solution.py:104
  25.8 0.8 fusion.7
  26.7 0.2 copy.48
  26.8 0.2 copy.49
  27.0 0.8 fusion.5
  27.9 0.2 copy.46
  28.0 0.2 copy.47
  28.9 1.1 copy.37
  29.9 0.9 convert_reduce_fusion
  30.8 0.5 multiply_cosine_fusion
  31.4 0.1 multiply_subtract_fusion
  31.5 0.1 maximum_convert_fusion
  31.6 0.1 copy.43
  31.8 0.9 fusion.13
  32.7 0.1 multiply_subtract_fusion.1
  32.8 0.4 select_reduce_fusion
  33.1 0.2 fusion.2
  33.3 0.3 fusion.1
  33.6 0.8 copy.40.oo_ref
  34.4 1.0 copy.42.os_ref
  35.4 1.0 copy.41.om_ref
  36.4 0.2 multiply_convert_fusion
  36.6 0.1 copy.33
  36.7 0.8 copy.39.q_ref
  37.6 0.8 copy.44
  38.4 0.7 fusion.17.alive_ref
  39.1 74.3 %all-gather.3.cloned.1.call-done = bf16[128,128,384]{2,1,0:T(8,128)(2,1)} async-done(((bf16[2,128,384]{2,1,0:T(8,128)(2,1)}), bf16[128,128,384]{2,1,0:T(8,128)(2,1)}) %all-gather.3.cloned.1.call-update) | async-done | bytes 12582928 | tf_op jit(solution)/shard_map/all_gather | solution.py:101
  113.4 13.8 %shard_map.104 = bf16[256,384]{1,0:T(8,128)(2,1)} custom-call(bf16[256,384]{1,0:T(8,128)(2,1)} %copy.39.q_ref, bf16[64,2,128,384]{3,2,1,0:T(8,128)(2,1)} %bitcast.25, bf16[64,2,128,384]{3,2,1,0:T(8,128)(2,1)} %bitcast.26, bf16[256,384]{1,0:T(8,128)(2,1)} %copy.40.oo_ref, f32[3,256,1]{2,1,0:T(8,128)} %copy.41.om_ref, f32[3,256,1]{2,1,0:T(8,128)} %copy.42.os_ref, ...), custom_call_target="tpu_custom_call" | custom-call | tf_op jit(solution)/shard_map/pallas_call | solution.py:69
  (8 shorter events, 0.1 us)
Async XLA Ops:
  7.2 106.2 %all-gather.3.cloned.1.call-start = ((), (), s32[]{:S(2)}) async-start(), calls=%async_computation | async-start | bytes 12779520 | tf_op jit(solution)/shard_map/all_gather | solution.py:101
Sparse Core Ops, SparseCore 0:
  11.9 101.4 all-gather.2

commit v4 on v3

--- a/solution.py
+++ b/solution.py
@@ -40,14 +40,17 @@
     return prefix_len + row_index - first_row
 
 
-def flash_kernel(q_ref, k_ref, v_ref, oo_ref, om_ref, os_ref, alive_ref, out_ref):
+def flash_kernel(q_ref, k_ref, v_ref, oo_ref, om_ref, os_ref, alive_ref, out_ref, *, scaling):
     keys = k_ref[...].reshape(-1, HD)
     vals = v_ref[...].reshape(-1, HD)
-    s = lax.dot_general(
-        q_ref[...],
-        keys,
-        (((1,), (1,)), ((), ())),
-        preferred_element_type=jnp.float32,
+    s = (
+        lax.dot_general(
+            q_ref[...],
+            keys,
+            (((1,), (1,)), ((), ())),
+            preferred_element_type=jnp.float32,
+        )
+        * scaling
     )
     m = jnp.max(s, axis=1, keepdims=True)
     p = jnp.exp(s - m)
@@ -63,11 +66,12 @@
     out_ref[...] = jnp.where(alive_ref[...] > 0.0, merged, 0.0).astype(out_ref.dtype)
 
 
-def prefix_attention(scaled_q2d, kv_rows, own_out2d, own_max, own_sum, alive_f, head_count):
-    row_count = scaled_q2d.shape[0]
+def prefix_attention(queries2d, kv_rows, own_out2d, own_max, own_sum, alive_f, head_count, scaling):
+    row_count = queries2d.shape[0]
     owners, _, shard_rows, _ = kv_rows.shape
+    kernel = lambda *refs: flash_kernel(*refs, scaling=scaling)
     return pl.pallas_call(
-        flash_kernel,
+        kernel,
         grid=(head_count,),
         in_specs=[
             pl.BlockSpec((row_count, HD), lambda h: (0, h)),
@@ -81,7 +85,7 @@
         out_specs=pl.BlockSpec((row_count, HD), lambda h: (0, h)),
         out_shape=jax.ShapeDtypeStruct((row_count, head_count * HD), jnp.bfloat16),
         compiler_params=pltpu.CompilerParams(dimension_semantics=("arbitrary",)),
-    )(scaled_q2d, kv_rows, kv_rows, own_out2d, own_max, own_sum, alive_f)
+    )(queries2d, kv_rows, kv_rows, own_out2d, own_max, own_sum, alive_f)
 
 
 def per_device(
@@ -112,8 +116,7 @@
     segment = segment_ids[0]
     live_count = live_rows[0]
     position = positions(segment, prefix_len)
-    rotated_q = rotate(normed_q.reshape(row_count, head_count, HD), position)
-    queries_bf = rotated_q.astype(jnp.bfloat16)
+    queries_bf = rotate(normed_q.reshape(row_count, head_count, HD), position).astype(jnp.bfloat16)
     rotated_k = rotate(normed_k.reshape(row_count, head_count, HD), position).astype(jnp.bfloat16)
     row_index = jnp.arange(row_count, dtype=jnp.int32)
     alive = row_index < live_count
@@ -139,15 +142,15 @@
         preferred_element_type=jnp.float32,
     )
     suffix_out = (summed / jnp.maximum(row_sum, 1.0).T[:, :, None]).astype(jnp.bfloat16)
-    scaled_q = (rotated_q * scaling).astype(jnp.bfloat16)
     attended = prefix_attention(
-        scaled_q.reshape(row_count, local_width),
+        queries_bf.reshape(row_count, local_width),
         kv_rows,
         suffix_out.reshape(row_count, local_width),
         row_best[:, :, None],
         row_sum[:, :, None],
         alive.astype(jnp.float32)[:, None],
         head_count,
+        scaling,
     )
     return (attended, suffix_cache.reshape(row_count, local_width))
 

time: 134 us -> 136 us (1.015)
    unnamed x8 -> x10, local copies, waits for them, and re-layouts: 4.68 us -> 4.68 us
  transfers between devices with their start and end apart: 1 -> 1, of which waited for: 1 -> 1; matrix products, arithmetic and copies ran while one was open for 11% -> 10% of each run, Pallas kernels for 0% -> 0%
where the time goes in v4:
time: 136 us; the launch traced here: 135 us
  waiting for transfers between devices  75.1 us (55%)
  Pallas kernels  15.1 us (11%)
  between operations  14.8 us (11%)
  blocking collectives  14.7 us (11%)
  local copies, waits for them, and re-layouts  8.61 us (6%)
  other arithmetic  6.32 us (5%)
    all_gather x1, waiting for transfers between devices, per_device(): kv_rows = lax.all_gather(kv_block, 'req', axis=0)  75.1 us
    pallas_call x1, Pallas kernels, prefix_attention(): pl.pallas_call(kernel, grid=(head_count,), in_specs=[pl.BlockSpec((row_co...  15.1 us
    psum x1, blocking collectives, per_device(): lax.psum((jnp.sum(query_f * query_f, axis=1), jnp.sum(key_f * key_f, axis...  14.7 us
    unnamed x10, local copies, waits for them, and re-layouts  4.68 us
  transfers between devices with their start and end apart: 1, of which 1 were waited for; matrix products, arithmetic and copies ran while one was open for 10% of the time, Pallas kernels for 0%

profile of v4, /device:TPU:1, one launch (start us, length us, event | category | flops | bytes accessed | tf_op | source)
XLA Modules:
  0.0 135.3 jit_solution(1833640698830846517)
XLA Ops:
  7.2 0.0 copy-start
  7.2 0.0 all-gather.3.cloned.1.call-start
  7.2 1.6 %pad_maximum_fusion = bf16[2,128,384]{2,1,0:T(8,128)(2,1)} fusion(bf16[1,128,384]{2,1,0:T(8,128)(2,1)} %bitcast.33, bf16[1,128,384]{2,1,0:T(8,128)(2,1)} %bitcast.34), kind=kLoop, calls=%fused_computation.29 | loop fusion | flops 98304 | bytes 393216 | tf_op jit(solution)/shard_map/stack | solution.py:104
  8.9 0.0 all-gather.3.cloned.1.call-update
  8.9 1.1 copy.34
  10.0 1.1 copy.30
  11.0 0.1 fusion.4
  11.1 0.1 fusion.6
  11.2 14.7 %all-reduce = (f32[256]{0:T(256)S(1)}, f32[256]{0:T(256)S(1)}) all-reduce(f32[256]{0:T(256)S(1)} %fusion.4, f32[256]{0:T(256)S(1)} %fusion.6), channel_id=1, replica_groups=mesh['req'=64,'pre'=8] {'pre'}, use_global_device_ids=true, to_apply=%region_1.0 | all-reduce | flops 512 | bytes 4096 | tf_op jit(solution)/shard_map/psum | solution.py:108
  25.9 0.8 fusion.7
  26.7 0.2 copy.49
  26.9 0.2 copy.48
  27.0 0.8 fusion.5
  27.9 0.2 copy.46
  28.0 0.2 copy.47
  28.2 0.9 convert_reduce_fusion
  29.1 0.5 multiply_cosine_fusion
  29.7 0.2 multiply_subtract_fusion
  29.9 0.1 maximum_convert_fusion
  30.0 0.1 copy.33
  30.2 0.8 copy.39.refs_0_
  31.0 1.1 copy.37
  32.7 0.1 maximum_convert_fusion.1
  32.8 0.1 copy.43
  33.0 0.0 copy-done
  33.0 0.1 fusion.13
  33.1 0.3 select_reduce_fusion
  33.5 0.2 fusion.2
  33.7 0.3 fusion.1
  34.0 0.8 copy.40.refs_3_
  34.8 1.0 copy.41.refs_4_
  35.8 1.0 copy.42.refs_5_
  36.8 0.8 copy.44
  37.6 0.7 fusion.16.refs_6_
  38.3 75.1 %all-gather.3.cloned.1.call-done = bf16[128,128,384]{2,1,0:T(8,128)(2,1)} async-done(((bf16[2,128,384]{2,1,0:T(8,128)(2,1)}), bf16[128,128,384]{2,1,0:T(8,128)(2,1)}) %all-gather.3.cloned.1.call-update) | async-done | bytes 12582928 | tf_op jit(solution)/shard_map/all_gather | solution.py:105
  113.4 15.1 %shard_map.104 = bf16[256,384]{1,0:T(8,128)(2,1)} custom-call(bf16[256,384]{1,0:T(8,128)(2,1)} %copy.39.refs_0_, bf16[64,2,128,384]{3,2,1,0:T(8,128)(2,1)} %bitcast.26, bf16[64,2,128,384]{3,2,1,0:T(8,128)(2,1)} %bitcast.27, bf16[256,384]{1,0:T(8,128)(2,1)} %copy.40.refs_3_, f32[3,256,1]{2,1,0:T(8,128)} %copy.41.refs_4_, f32[3,256,1]{2,1,0:T(8,128)} %copy.42.refs_5_, ...), custom_call_target="tpu_custom_call" | custom-call | tf_op jit(solution)/shard_map/pallas_call | solution.py:73
  (8 shorter events, 0.1 us)
Async XLA Ops:
  7.2 25.8 %copy-start = (s32[1,256]{1,0:T(1,128)S(1)}, s32[1,256]{1,0:T(1,128)}, u32[]{:S(2)}) copy-start(s32[1,256]{1,0:T(1,128)} %param.16) | copy-start | bytes 3076
  7.2 106.2 %all-gather.3.cloned.1.call-start = ((), (), s32[]{:S(2)}) async-start(), calls=%async_computation | async-start | bytes 12779520 | tf_op jit(solution)/shard_map/all_gather | solution.py:105
Sparse Core Ops, SparseCore 0:
  11.9 101.4 all-gather.2

commit v5 on v4

--- a/solution.py
+++ b/solution.py
@@ -88,6 +88,25 @@
     )(queries2d, kv_rows, kv_rows, own_out2d, own_max, own_sum, alive_f)
 
 
+def stack_kernel(k_hbm, v_hbm, out_hbm, sems):
+    first = pltpu.make_async_copy(k_hbm, out_hbm.at[0], sems.at[0])
+    second = pltpu.make_async_copy(v_hbm, out_hbm.at[1], sems.at[1])
+    first.start()
+    second.start()
+    first.wait()
+    second.wait()
+
+
+def stack_pair(keys, vals):
+    return pl.pallas_call(
+        stack_kernel,
+        in_specs=[pl.BlockSpec(memory_space=pl.ANY), pl.BlockSpec(memory_space=pl.ANY)],
+        out_specs=pl.BlockSpec(memory_space=pl.ANY),
+        out_shape=jax.ShapeDtypeStruct((2,) + keys.shape, keys.dtype),
+        scratch_shapes=[pltpu.SemaphoreType.DMA((2,))],
+    )(keys, vals)
+
+
 def per_device(
     queries_raw,
     keys_raw,
@@ -101,7 +120,7 @@
 ):
     row_count, local_width = queries_raw.shape
     head_count = local_width // HD
-    kv_block = jnp.stack([prefix_keys, prefix_values], axis=0)
+    kv_block = stack_pair(prefix_keys, prefix_values)
     kv_rows = lax.all_gather(kv_block, "req", axis=0)
     query_f = queries_raw.astype(jnp.float32)
     key_f = keys_raw.astype(jnp.float32)

time: 136 us -> 138 us (1.015)
  Pallas kernels: 15.1 us -> 22.1 us
  waiting for transfers between devices: 75.1 us -> 72.2 us
  other arithmetic: 6.32 us -> 4.68 us
    pallas_call x0 -> x1, Pallas kernels: none -> 7.08 us  [stack_pair(): pl.pallas_call(stack_kernel, in_specs=[pl.BlockSpec(memory_space=pl.ANY),...]
    all_gather x1, waiting for transfers between devices: 75.1 us -> 72.1 us  [per_device(): kv_rows = lax.all_gather(kv_block, 'req', axis=0)]
    another operation x1 -> x0, other arithmetic: 1.64 us -> none  [per_device(): kv_block = jnp.stack([prefix_keys, prefix_values], axis=0)]
where the time goes in v5:
time: 138 us
  waiting for transfers between devices  72.2 us (52%)
  Pallas kernels  22.1 us (16%)
  between operations  14.8 us (11%)
  blocking collectives  14.7 us (11%)
  local copies, waits for them, and re-layouts  8.61 us (6%)
  other arithmetic  4.68 us (3%)
    all_gather x1, waiting for transfers between devices, per_device(): kv_rows = lax.all_gather(kv_block, 'req', axis=0)  72.1 us
    pallas_call x1, Pallas kernels, prefix_attention(): pl.pallas_call(kernel, grid=(head_count,), in_specs=[pl.BlockSpec((row_co...  15 us
    psum x1, blocking collectives, per_device(): lax.psum((jnp.sum(query_f * query_f, axis=1), jnp.sum(key_f * key_f, axis...  14.7 us
    pallas_call x1, Pallas kernels, stack_pair(): pl.pallas_call(stack_kernel, in_specs=[pl.BlockSpec(memory_space=pl.ANY),...  7.08 us
    unnamed x10, local copies, waits for them, and re-layouts  4.68 us
  transfers between devices with their start and end apart: 1, of which 1 were waited for; matrix products, arithmetic and copies ran while one was open for 10% of the time, Pallas kernels for 0%

profile of v5, /device:TPU:1, one launch (start us, length us, event | category | flops | bytes accessed | tf_op | source)
XLA Modules:
  0.0 137.7 jit_solution(9941068724851750432)
XLA Ops:
  7.2 0.0 copy-start
  7.2 0.0 all-gather.3.cloned.1.call-start
  7.2 7.1 %shard_map.104 = bf16[2,128,384]{2,1,0:T(8,128)(2,1)} custom-call(bf16[128,384]{1,0:T(8,128)(2,1)} %k_hbm.1, bf16[128,384]{1,0:T(8,128)(2,1)} %v_hbm.1), custom_call_target="tpu_custom_call" | custom-call | tf_op jit(solution)/shard_map/pallas_call | solution.py:101
  14.3 0.0 all-gather.3.cloned.1.call-update
  14.3 1.1 copy.34
  15.4 1.1 copy.30
  16.5 0.1 fusion.4
  16.5 0.1 fusion.6
  16.6 14.7 %all-reduce = (f32[256]{0:T(256)S(1)}, f32[256]{0:T(256)S(1)}) all-reduce(f32[256]{0:T(256)S(1)} %fusion.4, f32[256]{0:T(256)S(1)} %fusion.6), channel_id=1, replica_groups=mesh['req'=64,'pre'=8] {'pre'}, use_global_device_ids=true, to_apply=%region_1.0 | all-reduce | flops 512 | bytes 4096 | tf_op jit(solution)/shard_map/psum | solution.py:127
  31.3 0.8 fusion.7
  32.1 0.2 copy.49
  32.3 0.2 copy.48
  32.5 0.8 fusion.5
  33.3 0.2 copy.46
  33.5 0.2 copy.47
  33.7 0.9 convert_reduce_fusion
  34.6 0.5 multiply_cosine_fusion
  35.1 0.2 multiply_subtract_fusion
  35.3 0.1 maximum_convert_fusion
  35.5 0.1 copy.33
  35.6 0.8 copy.39.refs_0_
  36.4 1.1 copy.37
  38.1 0.1 maximum_convert_fusion.1
  38.3 0.1 copy.43
  38.4 0.0 copy-done
  38.5 0.1 fusion.13
  38.6 0.3 select_reduce_fusion
  38.9 0.2 fusion.2
  39.1 0.3 fusion.1
  39.4 0.8 copy.40.refs_3_
  40.2 1.0 copy.41.refs_4_
  41.2 1.0 copy.42.refs_5_
  42.2 0.8 copy.44
  43.0 0.7 fusion.16.refs_6_
  43.7 72.1 %all-gather.3.cloned.1.call-done = bf16[128,128,384]{2,1,0:T(8,128)(2,1)} async-done(((bf16[2,128,384]{2,1,0:T(8,128)(2,1)}), bf16[128,128,384]{2,1,0:T(8,128)(2,1)}) %all-gather.3.cloned.1.call-update) | async-done | bytes 12582928 | tf_op jit(solution)/shard_map/all_gather | solution.py:124
  115.8 15.0 %shard_map.105 = bf16[256,384]{1,0:T(8,128)(2,1)} custom-call(bf16[256,384]{1,0:T(8,128)(2,1)} %copy.39.refs_0_, bf16[64,2,128,384]{3,2,1,0:T(8,128)(2,1)} %bitcast.24, bf16[64,2,128,384]{3,2,1,0:T(8,128)(2,1)} %bitcast.25, bf16[256,384]{1,0:T(8,128)(2,1)} %copy.40.refs_3_, f32[3,256,1]{2,1,0:T(8,128)} %copy.41.refs_4_, f32[3,256,1]{2,1,0:T(8,128)} %copy.42.refs_5_, ...), custom_call_target="tpu_custom_call" | custom-call | tf_op jit(solution)/shard_map/pallas_call | solution.py:73
  (8 shorter events, 0.1 us)
Async XLA Ops:
  7.2 31.3 %copy-start = (s32[1,256]{1,0:T(1,128)S(1)}, s32[1,256]{1,0:T(1,128)}, u32[]{:S(2)}) copy-start(s32[1,256]{1,0:T(1,128)} %param.16) | copy-start | bytes 3076
  7.2 108.7 %all-gather.3.cloned.1.call-start = ((), (), s32[]{:S(2)}) async-start(), calls=%async_computation | async-start | bytes 12779520 | tf_op jit(solution)/shard_map/all_gather | solution.py:124
Sparse Core Ops, SparseCore 0:
  14.5 101.3 all-gather.2

commit v6 on v4

--- a/solution.py
+++ b/solution.py
@@ -8,6 +8,7 @@
 from jax.sharding import PartitionSpec as P
 
 HD = 128
+LOG2_E = 1.4426950408889634
 
 
 epsilon = 1e-06
@@ -43,17 +44,15 @@
 def flash_kernel(q_ref, k_ref, v_ref, oo_ref, om_ref, os_ref, alive_ref, out_ref, *, scaling):
     keys = k_ref[...].reshape(-1, HD)
     vals = v_ref[...].reshape(-1, HD)
-    s = (
-        lax.dot_general(
-            q_ref[...],
-            keys,
-            (((1,), (1,)), ((), ())),
-            preferred_element_type=jnp.float32,
-        )
-        * scaling
+    s = lax.dot_general(
+        q_ref[...],
+        keys,
+        (((1,), (1,)), ((), ())),
+        preferred_element_type=jnp.float32,
     )
-    m = jnp.max(s, axis=1, keepdims=True)
-    p = jnp.exp(s - m)
+    top = jnp.max(s, axis=1, keepdims=True)
+    p = jnp.exp2((s - top) * (scaling * LOG2_E))
+    m = top * scaling
     prefix_sum = jnp.sum(p, axis=1, keepdims=True)
     prefix_acc = jnp.dot(p.astype(jnp.bfloat16), vals, preferred_element_type=jnp.float32)
     own_max = om_ref[...]

time: 136 us -> 135 us (level)
  no operation moved by 1% of the time
where the time goes in v6:
time: 135 us; the launch traced here: 134 us
  waiting for transfers between devices  75.1 us (56%)
  between operations  14.8 us (11%)
  blocking collectives  14.7 us (11%)
  Pallas kernels  14 us (10%)
  local copies, waits for them, and re-layouts  8.61 us (6%)
  other arithmetic  6.32 us (5%)
    all_gather x1, waiting for transfers between devices, per_device(): kv_rows = lax.all_gather(kv_block, 'req', axis=0)  75.1 us
    psum x1, blocking collectives, per_device(): lax.psum((jnp.sum(query_f * query_f, axis=1), jnp.sum(key_f * key_f, axis...  14.7 us
    pallas_call x1, Pallas kernels, prefix_attention(): pl.pallas_call(kernel, grid=(head_count,), in_specs=[pl.BlockSpec((row_co...  14 us
    unnamed x10, local copies, waits for them, and re-layouts  4.68 us
  transfers between devices with their start and end apart: 1, of which 1 were waited for; matrix products, arithmetic and copies ran while one was open for 10% of the time, Pallas kernels for 0%

profile of v6, /device:TPU:1, one launch (start us, length us, event | category | flops | bytes accessed | tf_op | source)
XLA Modules:
  0.0 134.3 jit_solution(10851111843879233926)
XLA Ops:
  7.2 0.0 copy-start
  7.2 0.0 all-gather.3.cloned.1.call-start
  7.2 1.6 %pad_maximum_fusion = bf16[2,128,384]{2,1,0:T(8,128)(2,1)} fusion(bf16[1,128,384]{2,1,0:T(8,128)(2,1)} %bitcast.33, bf16[1,128,384]{2,1,0:T(8,128)(2,1)} %bitcast.34), kind=kLoop, calls=%fused_computation.29 | loop fusion | flops 98304 | bytes 393216 | tf_op jit(solution)/shard_map/stack | solution.py:103
  8.9 0.0 all-gather.3.cloned.1.call-update
  8.9 1.1 copy.34
  10.0 1.1 copy.30
  11.0 0.1 fusion.4
  11.1 0.1 fusion.6
  11.2 14.7 %all-reduce = (f32[256]{0:T(256)S(1)}, f32[256]{0:T(256)S(1)}) all-reduce(f32[256]{0:T(256)S(1)} %fusion.4, f32[256]{0:T(256)S(1)} %fusion.6), channel_id=1, replica_groups=mesh['req'=64,'pre'=8] {'pre'}, use_global_device_ids=true, to_apply=%region_1.0 | all-reduce | flops 512 | bytes 4096 | tf_op jit(solution)/shard_map/psum | solution.py:107
  25.9 0.8 fusion.7
  26.7 0.2 copy.49
  26.9 0.2 copy.48
  27.0 0.8 fusion.5
  27.9 0.2 copy.46
  28.0 0.2 copy.47
  28.2 0.9 convert_reduce_fusion
  29.1 0.5 multiply_cosine_fusion
  29.7 0.2 multiply_subtract_fusion
  29.9 0.1 maximum_convert_fusion
  30.0 0.1 copy.33
  30.2 0.8 copy.39.refs_0_
  31.0 1.1 copy.37
  32.7 0.1 maximum_convert_fusion.1
  32.8 0.1 copy.43
  33.0 0.0 copy-done
  33.0 0.1 fusion.13
  33.1 0.3 select_reduce_fusion
  33.5 0.2 fusion.2
  33.7 0.3 fusion.1
  34.0 0.8 copy.40.refs_3_
  34.8 1.0 copy.41.refs_4_
  35.8 1.0 copy.42.refs_5_
  36.8 0.8 copy.44
  37.6 0.7 fusion.16.refs_6_
  38.3 75.1 %all-gather.3.cloned.1.call-done = bf16[128,128,384]{2,1,0:T(8,128)(2,1)} async-done(((bf16[2,128,384]{2,1,0:T(8,128)(2,1)}), bf16[128,128,384]{2,1,0:T(8,128)(2,1)}) %all-gather.3.cloned.1.call-update) | async-done | bytes 12582928 | tf_op jit(solution)/shard_map/all_gather | solution.py:104
  113.4 14.0 %shard_map.104 = bf16[256,384]{1,0:T(8,128)(2,1)} custom-call(bf16[256,384]{1,0:T(8,128)(2,1)} %copy.39.refs_0_, bf16[64,2,128,384]{3,2,1,0:T(8,128)(2,1)} %bitcast.26, bf16[64,2,128,384]{3,2,1,0:T(8,128)(2,1)} %bitcast.27, bf16[256,384]{1,0:T(8,128)(2,1)} %copy.40.refs_3_, f32[3,256,1]{2,1,0:T(8,128)} %copy.41.refs_4_, f32[3,256,1]{2,1,0:T(8,128)} %copy.42.refs_5_, ...), custom_call_target="tpu_custom_call" | custom-call | tf_op jit(solution)/shard_map/pallas_call | solution.py:72
  (8 shorter events, 0.1 us)
Async XLA Ops:
  7.2 25.8 %copy-start = (s32[1,256]{1,0:T(1,128)S(1)}, s32[1,256]{1,0:T(1,128)}, u32[]{:S(2)}) copy-start(s32[1,256]{1,0:T(1,128)} %param.16) | copy-start | bytes 3076
  7.2 106.2 %all-gather.3.cloned.1.call-start = ((), (), s32[]{:S(2)}) async-start(), calls=%async_computation | async-start | bytes 12779520 | tf_op jit(solution)/shard_map/all_gather | solution.py:104
Sparse Core Ops, SparseCore 0:
  11.9 101.4 all-gather.2

commit v7 on v6

--- a/solution.py
+++ b/solution.py
@@ -100,7 +100,11 @@
 ):
     row_count, local_width = queries_raw.shape
     head_count = local_width // HD
-    kv_block = jnp.stack([prefix_keys, prefix_values], axis=0)
+    kv_block = lax.select(
+        jnp.broadcast_to((jnp.arange(2) == 0)[:, None, None], (2,) + prefix_keys.shape),
+        jnp.broadcast_to(prefix_keys[None], (2,) + prefix_keys.shape),
+        jnp.broadcast_to(prefix_values[None], (2,) + prefix_keys.shape),
+    )
     kv_rows = lax.all_gather(kv_block, "req", axis=0)
     query_f = queries_raw.astype(jnp.float32)
     key_f = keys_raw.astype(jnp.float32)

time: 135 us -> 134 us (level)
    select_n x0 -> x1, other arithmetic: none -> 1.71 us  [per_device(): lax.select(jnp.broadcast_to((jnp.arange(2) == 0)[:, None, None], (2,) + p...]
    another operation x1 -> x0, other arithmetic: 1.64 us -> none  [per_device(): kv_block = jnp.stack([prefix_keys, prefix_values], axis=0)]
where the time goes in v7:
time: 134 us
  waiting for transfers between devices  75 us (56%)
  between operations  14.8 us (11%)
  blocking collectives  14.7 us (11%)
  Pallas kernels  14 us (10%)
  local copies, waits for them, and re-layouts  8.61 us (6%)
  other arithmetic  6.39 us (5%)
    all_gather x1, waiting for transfers between devices, per_device(): kv_rows = lax.all_gather(kv_block, 'req', axis=0)  75 us
    psum x1, blocking collectives, per_device(): lax.psum((jnp.sum(query_f * query_f, axis=1), jnp.sum(key_f * key_f, axis...  14.7 us
    pallas_call x1, Pallas kernels, prefix_attention(): pl.pallas_call(kernel, grid=(head_count,), in_specs=[pl.BlockSpec((row_co...  14 us
    unnamed x10, local copies, waits for them, and re-layouts  4.68 us
  transfers between devices with their start and end apart: 1, of which 1 were waited for; matrix products, arithmetic and copies ran while one was open for 10% of the time, Pallas kernels for 0%

profile of v7, /device:TPU:1, one launch (start us, length us, event | category | flops | bytes accessed | tf_op | source)
XLA Modules:
  0.0 134.2 jit_solution(3875837938798401908)
XLA Ops:
  7.2 0.0 copy-start
  7.2 0.0 all-gather.2.cloned.1.call-start
  7.2 1.7 %broadcast_select_fusion = bf16[1,2,128,384]{3,2,1,0:T(8,128)(2,1)} fusion(pred[2]{0:T(512)(128)(4,1)S(1)} %iota_compare_fusion.3, bf16[128,384]{1,0:T(8,128)(2,1)} %param.15, bf16[128,384]{1,0:T(8,128)(2,1)} %param.14), kind=kLoop, calls=%fused_computation.32 | loop fusion | flops 98304 | bytes 393218 | tf_op jit(solution)/shard_map/select_n | solution.py:103
  8.9 0.0 all-gather.2.cloned.1.call-update
  9.0 1.1 copy.34
  10.0 1.1 copy.30
  11.1 0.1 fusion.4
  11.2 0.1 fusion.6
  11.3 14.7 %all-reduce = (f32[256]{0:T(256)S(1)}, f32[256]{0:T(256)S(1)}) all-reduce(f32[256]{0:T(256)S(1)} %fusion.4, f32[256]{0:T(256)S(1)} %fusion.6), channel_id=1, replica_groups=mesh['req'=64,'pre'=8] {'pre'}, use_global_device_ids=true, to_apply=%region_1.0 | all-reduce | flops 512 | bytes 4096 | tf_op jit(solution)/shard_map/psum | solution.py:111
  25.9 0.8 fusion.7
  26.8 0.2 copy.49
  26.9 0.2 copy.48
  27.1 0.8 fusion.5
  28.0 0.2 copy.46
  28.1 0.2 copy.47
  28.3 0.9 convert_reduce_fusion
  29.2 0.5 multiply_cosine_fusion
  29.7 0.2 multiply_subtract_fusion
  30.0 0.1 maximum_convert_fusion
  30.1 0.1 copy.33
  30.2 0.8 copy.39.refs_0_
  31.1 1.1 copy.37
  32.8 0.1 maximum_convert_fusion.1
  32.9 0.1 copy.43
  33.1 0.0 copy-done
  33.1 0.1 fusion.13
  33.2 0.3 select_reduce_fusion
  33.6 0.2 fusion.2
  33.7 0.3 fusion.1
  34.1 0.8 copy.40.refs_3_
  34.9 1.0 copy.41.refs_4_
  35.8 1.0 copy.42.refs_5_
  36.9 0.8 copy.44
  37.7 0.7 fusion.16.refs_6_
  38.3 75.0 %all-gather.2.cloned.1.call-done.refs_1_.refs_2_ = bf16[64,2,128,384]{3,2,1,0:T(8,128)(2,1)} async-done(((bf16[1,2,128,384]{3,2,1,0:T(8,128)(2,1)}), bf16[64,2,128,384]{3,2,1,0:T(8,128)(2,1)}) %all-gather.2.cloned.1.call-update) | async-done | bytes 12582928 | tf_op jit(solution)/shard_map/all_gather | solution.py:108
  113.3 14.0 %shard_map.104 = bf16[256,384]{1,0:T(8,128)(2,1)} custom-call(bf16[256,384]{1,0:T(8,128)(2,1)} %copy.39.refs_0_, bf16[64,2,128,384]{3,2,1,0:T(8,128)(2,1)} %all-gather.2.cloned.1.call-done.refs_1_.refs_2_, bf16[64,2,128,384]{3,2,1,0:T(8,128)(2,1)} %all-gather.2.cloned.1.call-done.refs_1_.refs_2_, bf16[256,384]{1,0:T(8,128)(2,1)} %copy.40.refs_3_, ...), custom_call_target="tpu_custom_call" | custom-call | tf_op jit(solution)/shard_map/pallas_call | solution.py:72
  (9 shorter events, 0.1 us)
Async XLA Ops:
  7.2 25.9 %copy-start = (s32[1,256]{1,0:T(1,128)S(1)}, s32[1,256]{1,0:T(1,128)}, u32[]{:S(2)}) copy-start(s32[1,256]{1,0:T(1,128)} %param.16) | copy-start | bytes 3076
  7.2 106.1 %all-gather.2.cloned.1.call-start = ((), (), s32[]{:S(2)}) async-start(), calls=%async_computation | async-start | bytes 12779520 | tf_op jit(solution)/shard_map/all_gather | solution.py:108
Sparse Core Ops, SparseCore 0:
  11.9 101.3 all-gather.1

commit v8 on v6

--- a/solution.py
+++ b/solution.py
@@ -41,50 +41,50 @@
     return prefix_len + row_index - first_row
 
 
-def flash_kernel(q_ref, k_ref, v_ref, oo_ref, om_ref, os_ref, alive_ref, out_ref, *, scaling):
+def flash_kernel(qt_ref, k_ref, v_ref, oo_ref, om_ref, os_ref, alive_ref, out_ref, *, scaling):
     keys = k_ref[...].reshape(-1, HD)
     vals = v_ref[...].reshape(-1, HD)
-    s = lax.dot_general(
-        q_ref[...],
-        keys,
-        (((1,), (1,)), ((), ())),
+    scores_t = jnp.dot(keys, qt_ref[...], preferred_element_type=jnp.float32)
+    top = jnp.max(scores_t, axis=0, keepdims=True)
+    probs_t = jnp.exp2((scores_t - top) * (scaling * LOG2_E))
+    prefix_sum = jnp.sum(probs_t, axis=0, keepdims=True)
+    prefix_acc = lax.dot_general(
+        vals,
+        probs_t.astype(jnp.bfloat16),
+        (((0,), (0,)), ((), ())),
         preferred_element_type=jnp.float32,
     )
-    top = jnp.max(s, axis=1, keepdims=True)
-    p = jnp.exp2((s - top) * (scaling * LOG2_E))
     m = top * scaling
-    prefix_sum = jnp.sum(p, axis=1, keepdims=True)
-    prefix_acc = jnp.dot(p.astype(jnp.bfloat16), vals, preferred_element_type=jnp.float32)
     own_max = om_ref[...]
     best = jnp.maximum(m, own_max)
     prefix_weight = jnp.exp(m - best)
     own_weight = os_ref[...] * jnp.exp(own_max - best)
     numerator = prefix_acc * prefix_weight + own_weight * oo_ref[...].astype(jnp.float32)
     denominator = prefix_sum * prefix_weight + own_weight
-    merged = numerator / denominator
-    out_ref[...] = jnp.where(alive_ref[...] > 0.0, merged, 0.0).astype(out_ref.dtype)
+    merged = jnp.where(alive_ref[...] > 0.0, numerator / denominator, 0.0)
+    out_ref[...] = merged.T.astype(out_ref.dtype)
 
 
-def prefix_attention(queries2d, kv_rows, own_out2d, own_max, own_sum, alive_f, head_count, scaling):
-    row_count = queries2d.shape[0]
+def prefix_attention(queries_t, kv_rows, own_out_t, own_max, own_sum, alive_f, head_count, scaling):
+    row_count = queries_t.shape[1]
     owners, _, shard_rows, _ = kv_rows.shape
     kernel = lambda *refs: flash_kernel(*refs, scaling=scaling)
     return pl.pallas_call(
         kernel,
         grid=(head_count,),
         in_specs=[
-            pl.BlockSpec((row_count, HD), lambda h: (0, h)),
+            pl.BlockSpec((HD, row_count), lambda h: (h, 0)),
             pl.BlockSpec((owners, None, shard_rows, HD), lambda h: (0, 0, 0, h)),
             pl.BlockSpec((owners, None, shard_rows, HD), lambda h: (0, 1, 0, h)),
-            pl.BlockSpec((row_count, HD), lambda h: (0, h)),
-            pl.BlockSpec((None, row_count, 1), lambda h: (h, 0, 0)),
-            pl.BlockSpec((None, row_count, 1), lambda h: (h, 0, 0)),
-            pl.BlockSpec((row_count, 1), lambda h: (0, 0)),
+            pl.BlockSpec((HD, row_count), lambda h: (h, 0)),
+            pl.BlockSpec((None, 1, row_count), lambda h: (h, 0, 0)),
+            pl.BlockSpec((None, 1, row_count), lambda h: (h, 0, 0)),
+            pl.BlockSpec((1, row_count), lambda h: (0, 0)),
         ],
         out_specs=pl.BlockSpec((row_count, HD), lambda h: (0, h)),
         out_shape=jax.ShapeDtypeStruct((row_count, head_count * HD), jnp.bfloat16),
         compiler_params=pltpu.CompilerParams(dimension_semantics=("arbitrary",)),
-    )(queries2d, kv_rows, kv_rows, own_out2d, own_max, own_sum, alive_f)
+    )(queries_t, kv_rows, kv_rows, own_out_t, own_max, own_sum, alive_f)
 
 
 def per_device(
@@ -135,19 +135,20 @@
     weights = jnp.exp(jnp.where(allowed[None], scores - row_best[..., None], floor_value))
     row_sum = jnp.sum(weights, axis=-1)
     summed = jnp.einsum(
-        "hqk,khd->qhd",
+        "hqk,khd->hdq",
         weights.astype(jnp.bfloat16),
         values_grid,
         preferred_element_type=jnp.float32,
     )
-    suffix_out = (summed / jnp.maximum(row_sum, 1.0).T[:, :, None]).astype(jnp.bfloat16)
+    suffix_out_t = (summed / jnp.maximum(row_sum, 1.0)[:, None, :]).astype(jnp.bfloat16)
+    queries_t = jnp.transpose(queries_bf, (1, 2, 0)).reshape(local_width, row_count)
     attended = prefix_attention(
-        queries_bf.reshape(row_count, local_width),
+        queries_t,
         kv_rows,
-        suffix_out.reshape(row_count, local_width),
-        row_best[:, :, None],
-        row_sum[:, :, None],
-        alive.astype(jnp.float32)[:, None],
+        suffix_out_t.reshape(local_width, row_count),
+        row_best[:, None, :],
+        row_sum[:, None, :],
+        alive.astype(jnp.float32)[None, :],
         head_count,
         scaling,
     )

time: 135 us -> 136 us (level)
  local copies, waits for them, and re-layouts: 8.61 us -> 6.89 us
    unnamed x10 -> x8, local copies, waits for them, and re-layouts: 4.68 us -> 4.68 us
where the time goes in v8:
time: 136 us; the launch traced here: 135 us
  waiting for transfers between devices  75.6 us (56%)
  Pallas kernels  15.1 us (11%)
  between operations  14.8 us (11%)
  blocking collectives  14.7 us (11%)
  other arithmetic  6.93 us (5%)
  local copies, waits for them, and re-layouts  6.89 us (5%)
  matrix products  1.36 us (1%)
    all_gather x1, waiting for transfers between devices, per_device(): kv_rows = lax.all_gather(kv_block, 'req', axis=0)  75.5 us
    pallas_call x1, Pallas kernels, prefix_attention(): pl.pallas_call(kernel, grid=(head_count,), in_specs=[pl.BlockSpec((HD, ro...  15.1 us
    psum x1, blocking collectives, per_device(): lax.psum((jnp.sum(query_f * query_f, axis=1), jnp.sum(key_f * key_f, axis...  14.7 us
    unnamed x8, local copies, waits for them, and re-layouts  4.68 us
  transfers between devices with their start and end apart: 1, of which 1 were waited for; matrix products, arithmetic and copies ran while one was open for 10% of the time, Pallas kernels for 0%

profile of v8, /device:TPU:1, one launch (start us, length us, event | category | flops | bytes accessed | tf_op | source)
XLA Modules:
  0.0 135.4 jit_solution(9333760678953582582)
XLA Ops:
  7.2 0.0 all-gather.3.cloned.1.call-start
  7.2 1.6 %pad_maximum_fusion.1 = bf16[2,128,384]{2,1,0:T(8,128)(2,1)} fusion(bf16[1,128,384]{2,1,0:T(8,128)(2,1)} %bitcast.26, bf16[1,128,384]{2,1,0:T(8,128)(2,1)} %bitcast.27), kind=kLoop, calls=%fused_computation.28 | loop fusion | flops 98304 | bytes 393216 | tf_op jit(solution)/shard_map/stack | solution.py:103
  8.9 0.0 all-gather.3.cloned.1.call-update
  8.9 1.1 copy.25
  9.9 1.1 copy.29
  11.0 0.1 fusion.3
  11.1 0.1 fusion.5
  11.2 14.7 %all-reduce = (f32[256]{0:T(256)S(1)}, f32[256]{0:T(256)S(1)}) all-reduce(f32[256]{0:T(256)S(1)} %fusion.3, f32[256]{0:T(256)S(1)} %fusion.5), channel_id=1, replica_groups=mesh['req'=64,'pre'=8] {'pre'}, use_global_device_ids=true, to_apply=%region_1.0 | all-reduce | flops 512 | bytes 4096 | tf_op jit(solution)/shard_map/psum | solution.py:107
  25.8 0.8 fusion.6
  26.7 0.2 copy.39
  26.8 0.2 copy.40
  27.0 0.8 fusion.4
  27.9 0.2 copy.37
  28.0 0.2 copy.38
  28.9 1.1 copy.32
  29.9 0.9 convert_reduce_fusion
  30.8 0.5 multiply_cosine_fusion
  31.4 0.1 multiply_subtract_fusion
  31.5 0.1 maximum_convert_fusion
  31.6 0.1 copy.34
  31.8 0.9 fusion.12
  32.7 0.1 subtract_convert_fusion
  32.8 0.4 select_reduce_fusion
  33.2 0.6 broadcast_in_dim.36.refs_4_
  33.8 0.2 fusion.1
  33.9 0.6 reduce_sum.42.refs_5_
  34.5 0.1 fusion.16
  34.6 0.8 copy.28
  35.5 0.8 copy.35
  36.3 0.5 compare_convert_fusion.refs_6_
  36.9 1.0 fusion
  37.9 75.5 %all-gather.3.cloned.1.call-done = bf16[128,128,384]{2,1,0:T(8,128)(2,1)} async-done(((bf16[2,128,384]{2,1,0:T(8,128)(2,1)}), bf16[128,128,384]{2,1,0:T(8,128)(2,1)}) %all-gather.3.cloned.1.call-update) | async-done | bytes 12582928 | tf_op jit(solution)/shard_map/all_gather | solution.py:104
  113.4 15.1 %shard_map.104 = bf16[256,384]{1,0:T(8,128)(2,1)} custom-call(bf16[384,256]{1,0:T(8,128)(2,1)} %bitcast.23, bf16[64,2,128,384]{3,2,1,0:T(8,128)(2,1)} %bitcast.19, bf16[64,2,128,384]{3,2,1,0:T(8,128)(2,1)} %bitcast.20, bf16[384,256]{1,0:T(8,128)(2,1)} %bitcast.24, f32[3,1,256]{2,1,0:T(1,128)} %broadcast_in_dim.36.refs_4_, f32[3,1,256]{2,1,0:T(1,128)} %reduce_sum.42.refs_5_, ...), custom_call_target="tpu_custom_call" | custom-call | tf_op jit(solution)/shard_map/pallas_call | solution.py:72
  (8 shorter events, 0.1 us)
Async XLA Ops:
  7.2 106.2 %all-gather.3.cloned.1.call-start = ((), (), s32[]{:S(2)}) async-start(), calls=%async_computation | async-start | bytes 12779520 | tf_op jit(solution)/shard_map/all_gather | solution.py:104
Sparse Core Ops, SparseCore 0:
  11.9 101.4 all-gather.2
